TPU v7x, 256 devices: a whole 4x4x8 slice. The times are simulated.
256 devices in a mesh: seq: 256 (over y, z, x, core).
Axes of the slice: x: 4, y: 4, z: 8, core: 2. Of those that a mesh axis runs over, the one named last changes fastest.
Arguments:
- tokens: bfloat16 [131072, 192], P('seq'), may hold values from -6 to 6
- out_grad: bfloat16 [131072, 192], P('seq'), may hold values from -6 to 6
- spread_weight: bfloat16 [384, 768], replicated, may hold values from -0.3125 to 0.3125
- merge_weight: bfloat16 [768, 384], replicated, may hold values from -0.21875 to 0.21875
- switch_bias: float32 [384], replicated, may hold values from -4 to 4
- gate_logit: float32 [384], replicated, may hold values from -1 to 3
Outputs:
- network_out: bfloat16 [131072, 192], P('seq')
- token_grad: bfloat16 [131072, 192], P('seq')
- spread_grad: float32 [384, 768], replicated
- merge_grad: float32 [768, 384], replicated
- bias_grad: float32 [384], replicated
- gate_grad: float32 [384], replicated
All inputs are finite; a program needn't handle non-finite values.
Results may differ from a plain program's by a relative error of at most 0.008.
Values may be sent and summed in bfloat16 or wider, within the bound.
No kernel may reach another device: no remote copies, remote signals or barrier semaphores. Data moves between devices by JAX's collectives and lax.ppermute only.
A program may use at most 64 MiB of HBM per device.

v0:
```python
import math

import jax
import jax.numpy as jnp
from jax import lax
from jax.sharding import PartitionSpec as P

SECTIONS = 4


sqrt_half = 0.7071067811865476
inv_sqrt_two_pi = 0.3989422804014327


def swapped(value, axis, stride):
    mask = 2**stride
    pairs = [(source, source ^ mask) for source in range(lax.axis_size(axis))]
    return lax.ppermute(value, axis, pairs)


def gelu_exact(values):
    return 0.5 * values * (1.0 + lax.erf(values * sqrt_half))


def gelu_slope(values):
    return (
        0.5 * (1.0 + lax.erf(values * sqrt_half))
        + values * jnp.exp(-0.5 * values * values) * inv_sqrt_two_pi
    )


def normalize(pre_norm):
    centered = pre_norm - jnp.mean(pre_norm, -1, keepdims=True)
    inv_scale = lax.rsqrt(jnp.mean(centered * centered, -1, keepdims=True) + 1e-05)
    return (centered * inv_scale, inv_scale)


def switch_forward(paired, spread_weight, merge_weight, switch_bias, gate_logit):
    pre_norm = jnp.dot(paired, spread_weight, preferred_element_type=jnp.float32)
    normed, inv_scale = normalize(pre_norm)
    hidden = gelu_exact(normed).astype(jnp.bfloat16)
    branch = jnp.dot(hidden, merge_weight, preferred_element_type=jnp.float32) + switch_bias
    return (jax.nn.sigmoid(gate_logit) * paired.astype(jnp.float32) + 0.25 * branch).astype(
        jnp.bfloat16
    )


def switch_backward(paired, grad_pairs, spread_weight, merge_weight, gate_logit, row_mask):
    pre_norm = jnp.dot(paired, spread_weight, preferred_element_type=jnp.float32)
    normed, inv_scale = normalize(pre_norm)
    hidden = gelu_exact(normed).astype(jnp.bfloat16)
    grad_rows = grad_pairs.astype(jnp.float32)
    branch_grad = (0.25 * grad_rows).astype(jnp.bfloat16)
    hidden_grad = lax.dot_general(
        branch_grad, merge_weight, (((1,), (1,)), ((), ())), preferred_element_type=jnp.float32
    )
    normed_grad = hidden_grad * gelu_slope(normed)
    pre_grad = inv_scale * (
        normed_grad
        - jnp.mean(normed_grad, -1, keepdims=True)
        - normed * jnp.mean(normed_grad * normed, -1, keepdims=True)
    )
    pre_grad = pre_grad.astype(jnp.bfloat16)
    back_rows = lax.dot_general(
        pre_grad, spread_weight, (((1,), (1,)), ((), ())), preferred_element_type=jnp.float32
    )
    paired_grad = (jax.nn.sigmoid(gate_logit) * grad_rows + back_rows).astype(jnp.bfloat16)
    masked_grad = grad_rows * row_mask
    masked_branch = branch_grad * row_mask.astype(jnp.bfloat16)
    masked_pre = pre_grad * row_mask.astype(jnp.bfloat16)
    gate_term = jnp.sum(masked_grad * paired.astype(jnp.float32), 0)
    bias_term = 0.25 * jnp.sum(masked_grad, 0)
    merge_term = lax.dot_general(
        hidden, masked_branch, (((0,), (0,)), ((), ())), preferred_element_type=jnp.float32
    )
    spread_term = lax.dot_general(
        paired, masked_pre, (((0,), (0,)), ((), ())), preferred_element_type=jnp.float32
    )
    return (paired_grad, (spread_term, merge_term, bias_term, gate_term))


def on_device(tokens, out_grad, spread_weight, merge_weight, switch_bias, gate_logit):
    row_count, unit_count = tokens.shape
    half_rows = row_count // 2
    device_bits = lax.axis_size("seq").bit_length() - 1
    grad_scale = 1.0 / math.sqrt(lax.axis_size("seq") * row_count)
    position = lax.axis_index("seq")

    def upper_side(bit_num):
        return position // 2**bit_num % 2 == 1

    def gather_pairs(rows, bit_num):
        is_upper = upper_side(bit_num)
        incoming = swapped(rows.reshape(-1, 2 * unit_count), "seq", bit_num).reshape(
            row_count, unit_count
        )
        lower_rows = jnp.where(is_upper, incoming, rows)
        upper_rows = jnp.where(is_upper, rows, incoming)
        return jnp.concatenate([lower_rows, upper_rows], 1)

    def split_pairs(result, bit_num):
        is_upper = upper_side(bit_num)
        left_part = result[:, :unit_count]
        right_part = result[:, unit_count:]
        own_part = jnp.where(is_upper, right_part, left_part)
        return own_part

    spread_total = jnp.zeros(spread_weight.shape, jnp.float32)
    merge_total = jnp.zeros(merge_weight.shape, jnp.float32)
    bias_total = jnp.zeros(switch_bias.shape, jnp.float32)
    gate_total = jnp.zeros(gate_logit.shape, jnp.float32)
    saved = []
    current = tokens
    for section_num in range(SECTIONS):
        bit_num = device_bits - 1 - section_num
        paired = gather_pairs(current, bit_num)
        saved.append(paired)
        current = split_pairs(
            switch_forward(paired, spread_weight, merge_weight, switch_bias, gate_logit), bit_num
        )
    grad_rows = out_grad
    for section_num in reversed(range(SECTIONS)):
        bit_num = device_bits - 1 - section_num
        grad_pairs = gather_pairs(grad_rows, bit_num)
        term_is_upper = upper_side(bit_num)
        row_index = lax.broadcasted_iota(jnp.int32, (row_count, 1), 0)
        owned = jnp.where(term_is_upper, row_index >= half_rows, row_index < half_rows)
        row_mask = owned.astype(jnp.float32)
        paired_grad, term_list = switch_backward(
            saved[section_num], grad_pairs, spread_weight, merge_weight, gate_logit, row_mask
        )
        spread_total = spread_total + term_list[0]
        merge_total = merge_total + term_list[1]
        bias_total = bias_total + term_list[2]
        gate_total = gate_total + term_list[3]
        grad_rows = split_pairs(paired_grad, bit_num)
    spread_sum, merge_sum, bias_sum, gate_sum = lax.psum(
        (spread_total, merge_total, bias_total, gate_total), "seq"
    )
    gate_open = jax.nn.sigmoid(gate_logit)
    return (
        current,
        grad_rows,
        spread_sum * grad_scale,
        merge_sum * grad_scale,
        bias_sum * grad_scale,
        gate_sum * gate_open * (1.0 - gate_open) * grad_scale,
    )


def solution(mesh):
    placed = (P("seq", None), P("seq", None), P(), P(), P(), P())
    return jax.shard_map(
        on_device,
        mesh=mesh,
        in_specs=placed,
        out_specs=(P("seq", None), P("seq", None), P(), P(), P(), P()),
        check_vma=False,
    )
```

profile of v0, /device:TPU:32, one launch (start us, length us, event | category | flops | bytes accessed | tf_op | source)
XLA Modules:
  0.0 420.4 jit_solution(6988517575162472090)
XLA Ops:
  8.6 3.3 collective-permute-start
  13.8 3.3 collective-permute-start.4
  25.5 4.5 %collective-permute-done.1 = bf16[256,384]{1,0:T(8,128)(2,1)} collective-permute-done((bf16[256,384]{1,0:T(8,128)(2,1)}, bf16[256,384]{1,0:T(8,128)(2,1)}, u32[]{:S(2)}, u32[]{:S(2)}) %collective-permute-start.1) | collective-permute-done | bytes 196640 | tf_op jit(solution)/shard_map/ppermute | solution.py:18
  38.4 5.1 %collective-permute-start.2 = (bf16[256,384]{1,0:T(8,128)(2,1)}, bf16[256,384]{1,0:T(8,128)(2,1)}, u32[]{:S(2)}, u32[]{:S(2)}) collective-permute-start(bf16[256,384]{1,0:T(8,128)(2,1)} %reshape.186), channel_id=1, source_target_pairs={{0,32},{1,33},{2,34},{3,35},{4,36},{5,37},{6,38},{7,39},{8,40},{9,... | collective-permute-start | bytes 589832 | tf_op jit(solution)/shard_map/ppermute | solution.py:18
  44.6 7.5 %collective-permute-done.2 = bf16[256,384]{1,0:T(8,128)(2,1)} collective-permute-done((bf16[256,384]{1,0:T(8,128)(2,1)}, bf16[256,384]{1,0:T(8,128)(2,1)}, u32[]{:S(2)}, u32[]{:S(2)}) %collective-permute-start.2) | collective-permute-done | bytes 196640 | tf_op jit(solution)/shard_map/ppermute | solution.py:18
  62.5 3.8 collective-permute-done.3
  69.6 2.0 fusion.101
  78.4 1.8 copy.27
  80.2 1.8 reshape.192
  82.0 4.6 %collective-permute-start.5 = (bf16[256,384]{1,0:T(8,128)(2,1)}, bf16[256,384]{1,0:T(8,128)(2,1)}, u32[]{:S(2)}, u32[]{:S(2)}) collective-permute-start(bf16[256,384]{1,0:T(8,128)(2,1)} %reshape.192), channel_id=1, source_target_pairs={{0,32},{1,33},{2,34},{3,35},{4,36},{5,37},{6,38},{7,39},{8,40},{9,... | collective-permute-start | bytes 589832 | tf_op jit(solution)/shard_map/ppermute | solution.py:18
  89.9 2.1 collective-permute-done.5
  94.3 3.0 fusion.100
  100.7 1.8 copy.30
  102.5 1.8 reshape.194
  104.3 1.9 collective-permute-start.6
  106.2 3.1 convolution_add_fusion.2
  114.8 3.0 fusion.99
  122.9 1.8 reshape.196
  124.7 2.9 collective-permute-start.7
  127.7 3.3 convolution_add_fusion.1
  135.8 2.0 fusion.98
  144.0 82.1 %all-reduce = (f32[384]{0:T(512)S(1)}, f32[384]{0:T(512)S(1)}) all-reduce(f32[384]{0:T(512)S(1)} %add_multiply_fusion, f32[384]{0:T(512)S(1)} %add_add_fusion), channel_id=1, replica_groups=mesh['seq'=256] {'seq'}, use_global_device_ids=true, to_apply=%region_22.23 | all-reduce | flops 768 | bytes 6144 | tf_op jit(solution)/shard_map/psum | solution.py:137
  228.5 181.5 %all-reduce.4.cloned.1.call-done = (f32[384,768]{1,0:T(8,128)}, f32[768,384]{1,0:T(8,128)}) async-done(((f32[384,768]{1,0:T(8,128)}, f32[768,384]{1,0:T(8,128)}), (f32[384,768]{1,0:T(8,128)}, f32[768,384]{1,0:T(8,128)})) %all-reduce.4.cloned.1.call-update) | async-done | bytes 2359312 | tf_op jit(solution)/shard_map/psum | solution.py:137
  410.0 2.5 broadcast_multiply_fusion
  (268 shorter events, 74.9 us)
Async XLA Ops:
  7.2 13.3 %copy-start = (bf16[768,384]{1,0:T(8,128)(2,1)S(1)}, bf16[768,384]{1,0:T(8,128)(2,1)}, u32[]{:S(2)}) copy-start(bf16[768,384]{1,0:T(8,128)(2,1)} %param.9) | copy-start | bytes 1769476
  7.2 10.8 %copy-start.51 = (bf16[512,192]{0,1:T(8,128)(2,1)S(1)}, bf16[512,192]{0,1:T(8,128)(2,1)}, u32[]{:S(2)}) copy-start(bf16[512,192]{0,1:T(8,128)(2,1)} %param.6) | copy-start | bytes 589828
  7.2 10.5 %copy-start.66 = (f32[384]{0:T(512)S(1)}, f32[384]{0:T(512)}, u32[]{:S(2)}) copy-start(f32[384]{0:T(512)} %param.11) | copy-start | bytes 4612
  7.2 402.8 %all-reduce.4.cloned.1.call-start = ((), (), s32[]{:S(2)}) async-start(), calls=%async_computation | async-start | bytes 4718592 | tf_op jit(solution)/shard_map/psum | solution.py:137
  8.4 9.7 %copy-start.5 = (bf16[384,768]{1,0:T(8,128)(2,1)S(1)}, bf16[384,768]{1,0:T(8,128)(2,1)}, u32[]{:S(2)}) copy-start(bf16[384,768]{1,0:T(8,128)(2,1)} %param.8) | copy-start | bytes 1769476
  8.6 9.1 %collective-permute-start = (bf16[256,384]{1,0:T(8,128)(2,1)S(1)}, bf16[256,384]{1,0:T(8,128)(2,1)S(1)}, u32[]{:S(2)}, u32[]{:S(2)}) collective-permute-start(bf16[256,384]{1,0:T(8,128)(2,1)S(1)} %reshape.182), channel_id=1, source_target_pairs={{0,128},{1,129},{2,130},{3,131},{4,132},{5,133},{6,134},{7,135},{8... | collective-permute-start | bytes 589832 | tf_op jit(solution)/shard_map/ppermute | solution.py:18
  13.8 46.7 %collective-permute-start.4 = (bf16[256,384]{1,0:T(8,128)(2,1)}, bf16[256,384]{1,0:T(8,128)(2,1)}, u32[]{:S(2)}, u32[]{:S(2)}) collective-permute-start(bf16[256,384]{1,0:T(8,128)(2,1)} %reshape.190), channel_id=1, source_target_pairs={{0,16},{1,17},{2,18},{3,19},{4,20},{5,21},{6,22},{7,23},{8,24},{9,... | collective-permute-start | bytes 589832 | tf_op jit(solution)/shard_map/ppermute | solution.py:18
  17.7 38.8 %copy-start.71 = (f32[384]{0:T(512)}, f32[384]{0:T(512)S(1)}, u32[]{:S(2)}) copy-start(f32[384]{0:T(512)S(1)} %add_divide_fusion) | copy-start | bytes 4612
  23.6 6.4 %collective-permute-start.1 = (bf16[256,384]{1,0:T(8,128)(2,1)}, bf16[256,384]{1,0:T(8,128)(2,1)}, u32[]{:S(2)}, u32[]{:S(2)}) collective-permute-start(bf16[256,384]{1,0:T(8,128)(2,1)} %reshape.184), channel_id=1, source_target_pairs={{0,64},{1,65},{2,66},{3,67},{4,68},{5,69},{6,70},{7,71},{8,72},{9,... | collective-permute-start | bytes 589832 | tf_op jit(solution)/shard_map/ppermute | solution.py:18
  38.4 13.7 %collective-permute-start.2 = (bf16[256,384]{1,0:T(8,128)(2,1)}, bf16[256,384]{1,0:T(8,128)(2,1)}, u32[]{:S(2)}, u32[]{:S(2)}) collective-permute-start(bf16[256,384]{1,0:T(8,128)(2,1)} %reshape.186), channel_id=1, source_target_pairs={{0,32},{1,33},{2,34},{3,35},{4,36},{5,37},{6,38},{7,39},{8,40},{9,... | collective-permute-start | bytes 589832 | tf_op jit(solution)/shard_map/ppermute | solution.py:18
  58.9 7.4 %collective-permute-start.3 = (bf16[256,384]{1,0:T(8,128)(2,1)S(1)}, bf16[256,384]{1,0:T(8,128)(2,1)S(1)}, u32[]{:S(2)}, u32[]{:S(2)}) collective-permute-start(bf16[256,384]{1,0:T(8,128)(2,1)S(1)} %reshape.188), channel_id=1, source_target_pairs={{0,16},{1,17},{2,18},{3,19},{4,20},{5,21},{6,22},{7,23},{8,24},{9,... | collective-permute-start | bytes 589832 | tf_op jit(solution)/shard_map/ppermute | solution.py:18
  82.0 9.9 %collective-permute-start.5 = (bf16[256,384]{1,0:T(8,128)(2,1)}, bf16[256,384]{1,0:T(8,128)(2,1)}, u32[]{:S(2)}, u32[]{:S(2)}) collective-permute-start(bf16[256,384]{1,0:T(8,128)(2,1)} %reshape.192), channel_id=1, source_target_pairs={{0,32},{1,33},{2,34},{3,35},{4,36},{5,37},{6,38},{7,39},{8,40},{9,... | collective-permute-start | bytes 589832 | tf_op jit(solution)/shard_map/ppermute | solution.py:18
  98.7 7.5 %copy-start.15 = (bf16[512,768]{1,0:T(8,128)(2,1)S(1)}, bf16[512,768]{1,0:T(8,128)(2,1)}, u32[]{:S(2)}) copy-start(bf16[512,768]{1,0:T(8,128)(2,1)} %copy-done.14) | copy-start | bytes 2359300
  98.7 7.5 %copy-start.70 = (bf16[512]{0:T(512)(128)(2,1)S(1)}, bf16[512]{0:T(512)(128)(2,1)}, u32[]{:S(2)}) copy-start(bf16[512]{0:T(512)(128)(2,1)} %fusion.84) | copy-start | bytes 3076
  104.3 5.0 %copy-start.27 = (bf16[512,192]{0,1:T(8,128)(2,1)S(1)}, bf16[512,192]{0,1:T(8,128)(2,1)}, u32[]{:S(2)}) copy-start(bf16[512,192]{0,1:T(8,128)(2,1)} %copy-done.26) | copy-start | bytes 589828
  104.3 5.0 %copy-start.29 = (bf16[512,768]{1,0:T(8,128)(2,1)S(1)}, bf16[512,768]{1,0:T(8,128)(2,1)}, u32[]{:S(2)}) copy-start(bf16[512,768]{1,0:T(8,128)(2,1)} %copy-done.28) | copy-start | bytes 2359300
  104.3 7.5 %collective-permute-start.6 = (bf16[256,384]{1,0:T(8,128)(2,1)}, bf16[256,384]{1,0:T(8,128)(2,1)}, u32[]{:S(2)}, u32[]{:S(2)}) collective-permute-start(bf16[256,384]{1,0:T(8,128)(2,1)} %reshape.194), channel_id=1, source_target_pairs={{0,64},{1,65},{2,66},{3,67},{4,68},{5,69},{6,70},{7,71},{8,72},{9,... | collective-permute-start | bytes 589832 | tf_op jit(solution)/shard_map/ppermute | solution.py:18
  119.1 8.5 %copy-start.13 = (bf16[512,768]{1,0:T(8,128)(2,1)S(1)}, bf16[512,768]{1,0:T(8,128)(2,1)}, u32[]{:S(2)}) copy-start(bf16[512,768]{1,0:T(8,128)(2,1)} %copy-done.12) | copy-start | bytes 2359300
  119.1 8.5 %copy-start.56 = (bf16[512]{0:T(512)(128)(2,1)S(1)}, bf16[512]{0:T(512)(128)(2,1)}, u32[]{:S(2)}) copy-start(bf16[512]{0:T(512)(128)(2,1)} %get-tuple-element.57) | copy-start | bytes 3076
  124.7 8.1 %collective-permute-start.7 = (bf16[256,384]{1,0:T(8,128)(2,1)}, bf16[256,384]{1,0:T(8,128)(2,1)}, u32[]{:S(2)}, u32[]{:S(2)}) collective-permute-start(bf16[256,384]{1,0:T(8,128)(2,1)} %reshape.196), channel_id=1, source_target_pairs={{0,128},{1,129},{2,130},{3,131},{4,132},{5,133},{6,134},{7,135},{8... | collective-permute-start | bytes 589832 | tf_op jit(solution)/shard_map/ppermute | solution.py:18
  143.3 83.3 %copy-start.67 = (f32[384]{0:T(512)S(1)}, f32[384]{0:T(512)}, u32[]{:S(2)}) copy-start(f32[384]{0:T(512)} %param.11) | copy-start | bytes 4612
  143.3 83.9 %copy-start.33 = (bf16[512,192]{0,1:T(8,128)(2,1)S(1)}, bf16[512,192]{0,1:T(8,128)(2,1)}, u32[]{:S(2)}) copy-start(bf16[512,192]{0,1:T(8,128)(2,1)} %copy-done.32) | copy-start | bytes 589828
  143.3 83.9 %copy-start.35 = (bf16[512,192]{0,1:T(8,128)(2,1)S(1)}, bf16[512,192]{0,1:T(8,128)(2,1)}, u32[]{:S(2)}) copy-start(bf16[512,192]{0,1:T(8,128)(2,1)} %copy-done.34) | copy-start | bytes 589828
  143.3 83.9 %copy-start.75 = (f32[384]{0:T(512)S(1)}, f32[384]{0:T(512)}, u32[]{:S(2)}) copy-start(f32[384]{0:T(512)} %copy-done.71) | copy-start | bytes 4612
  (63 other events, 126.6 us)
Sparse Core Ops, SparseCore 0:
  143.5 266.4 all-reduce.3
where the time goes:
time: 424 us; the launch traced here: 420 us
  waiting for transfers between devices  199 us (47%)
  blocking collectives  82.1 us (19%)
  local copies, waits for them, and re-layouts  38.6 us (9%)
  matrix products  33.6 us (8%)
  other arithmetic  29.2 us (7%)
  starting transfers between devices  22.4 us (5%)
  between operations  15.2 us (4%)
    psum x1, waiting for transfers between devices, on_device(): lax.psum((spread_total, merge_total, bias_total, gate_total), 'seq')  181 us
    psum x1, blocking collectives, on_device(): lax.psum((spread_total, merge_total, bias_total, gate_total), 'seq')  82.1 us
    ppermute x8, starting transfers between devices, swapped(): return lax.ppermute(value, axis, pairs)  22.4 us
    ppermute x8, waiting for transfers between devices, swapped(): return lax.ppermute(value, axis, pairs)  17.8 us
    reshape x16, local copies, waits for them, and re-layouts, gather_pairs(): swapped(rows.reshape(-1, 2 * unit_count), 'seq', bit_num)  12.2 us
    unnamed x158, local copies, waits for them, and re-layouts  10.3 us
    dot_general x4, matrix products, switch_backward(): lax.dot_general(branch_grad, merge_weight, (((1,), (1,)), ((), ())), pref...  9.99 us
    dot_general x4, matrix products, switch_backward(): lax.dot_general(hidden, masked_branch, (((0,), (0,)), ((), ())), preferre...  9.62 us
  transfers between devices with their start and end apart: 9, of which 5 were waited for; matrix products, arithmetic and copies ran while one was open for 10% of the time, Pallas kernels for 0%

commit v1 on v0

v1 whole, which is shorter than its diff:
```python
import math

import jax
import jax.numpy as jnp
from jax import lax
from jax.experimental import pallas as pl
from jax.experimental.pallas import tpu as pltpu
from jax.sharding import PartitionSpec as P

SECTIONS = 4
MEMBERS = 16
ROWS = 32
UNITS = 192
SWITCH = 384
HIDDEN = 768
PAIRS = 256
CHUNK = 576
AUX = 8
SLOT = 24
BLOCK = 32

sqrt_half = 0.7071067811865476
inv_sqrt_two_pi = 0.3989422804014327
f32 = jnp.float32
bf16 = jnp.bfloat16


def dot(a, b, ca, cb):
    return lax.dot_general(a, b, (((ca,), (cb,)), ((), ())), preferred_element_type=f32)


def sides(section):
    bit = MEMBERS >> (section + 1)
    lower = [g for g in range(MEMBERS) if not g & bit]
    return lower, [g + bit for g in lower]


def load_rows(ref, members):
    return jnp.concatenate([ref[g] for g in members], 0)


def store_rows(ref, members, value):
    for k, g in enumerate(members):
        ref[g] = value[ROWS * k : ROWS * (k + 1)]


def switch_kernel(
    core,
    packed,
    spread,
    merge,
    bias,
    gate,
    packed_out,
    send,
    keep,
    state,
    grad,
    left,
    right,
    pre,
    normed,
    slope,
    hidden,
    scale,
    dbranch,
    dpre,
):
    gate_open = jax.nn.sigmoid(gate[...])
    gate_left = gate_open[:, :UNITS]
    gate_right = gate_open[:, UNITS:]
    bias_left = 0.25 * bias[:, :UNITS]
    bias_right = 0.25 * bias[:, UNITS:]
    state[...] = packed[:, :, :UNITS]
    grad[...] = packed[:, :, UNITS:]
    for section in range(SECTIONS):
        lower, upper = sides(section)
        base = PAIRS * section
        rows = slice(base, base + PAIRS)
        x_left = load_rows(state, lower)
        x_right = load_rows(state, upper)
        left[rows] = x_left
        right[rows] = x_right
        pre[...] = dot(x_left, spread[:UNITS, :], 1, 0) + dot(x_right, spread[UNITS:, :], 1, 0)

        def forward(block, carry, base=base):
            start = pl.multiple_of(block * BLOCK, BLOCK)
            at = pl.ds(start, BLOCK)
            to = pl.ds(base + start, BLOCK)
            value = pre[at, :]
            centered = value - jnp.mean(value, -1, keepdims=True)
            inv = lax.rsqrt(jnp.mean(centered * centered, -1, keepdims=True) + 1e-05)
            norm = centered * inv
            cdf = 0.5 * (1.0 + lax.erf(norm * sqrt_half))
            normed[to, :] = norm
            slope[to, :] = cdf + norm * jnp.exp(-0.5 * norm * norm) * inv_sqrt_two_pi
            hidden[to, :] = (norm * cdf).astype(bf16)
            scale[to, :] = jnp.broadcast_to(inv, (BLOCK, 128))
            return carry

        lax.fori_loop(0, PAIRS // BLOCK, forward, 0)
        act = hidden[rows, :]
        branch_left = dot(act, merge[:, :UNITS], 1, 0)
        branch_right = dot(act, merge[:, UNITS:], 1, 0)
        out_left = gate_left * x_left.astype(f32) + (0.25 * branch_left + bias_left)
        out_right = gate_right * x_right.astype(f32) + (0.25 * branch_right + bias_right)
        store_rows(state, lower, out_left.astype(bf16))
        store_rows(state, upper, out_right.astype(bf16))
    packed_out[:, :, :UNITS] = state[...]

    bias_sum = [jnp.zeros((1, UNITS), f32)] * 2
    gate_sum = [jnp.zeros((1, UNITS), f32)] * 2
    for section in reversed(range(SECTIONS)):
        lower, upper = sides(section)
        base = PAIRS * section
        rows = slice(base, base + PAIRS)
        d_left = load_rows(grad, lower)
        d_right = load_rows(grad, upper)
        wide_left = d_left.astype(f32)
        wide_right = d_right.astype(f32)
        bias_sum[0] += jnp.sum(wide_left, 0, keepdims=True)
        bias_sum[1] += jnp.sum(wide_right, 0, keepdims=True)
        gate_sum[0] += jnp.sum(wide_left * left[rows].astype(f32), 0, keepdims=True)
        gate_sum[1] += jnp.sum(wide_right * right[rows].astype(f32), 0, keepdims=True)
        b_left = (0.25 * wide_left).astype(bf16)
        b_right = (0.25 * wide_right).astype(bf16)
        dbranch[rows, :UNITS] = b_left
        dbranch[rows, UNITS:] = b_right
        pre[...] = dot(b_left, merge[:, :UNITS], 1, 1) + dot(b_right, merge[:, UNITS:], 1, 1)

        def backward(block, carry, base=base):
            start = pl.multiple_of(block * BLOCK, BLOCK)
            at = pl.ds(start, BLOCK)
            to = pl.ds(base + start, BLOCK)
            norm = normed[to, :]
            dn = pre[at, :] * slope[to, :]
            mean = jnp.mean(dn, -1, keepdims=True)
            along = jnp.mean(dn * norm, -1, keepdims=True)
            inv = scale[to, :][:, :1]
            dpre[to, :] = (inv * (dn - mean - norm * along)).astype(bf16)
            return carry

        lax.fori_loop(0, PAIRS // BLOCK, backward, 0)
        back = dpre[rows, :]
        g_left = gate_left * wide_left + dot(back, spread[:UNITS, :], 1, 1)
        g_right = gate_right * wide_right + dot(back, spread[UNITS:, :], 1, 1)
        store_rows(grad, lower, g_left.astype(bf16))
        store_rows(grad, upper, g_right.astype(bf16))
    packed_out[:, :, UNITS:] = grad[...]

    spread_terms = [dot(left[...], dpre[...], 0, 0), dot(right[...], dpre[...], 0, 0)]
    merge_term = dot(hidden[...], dbranch[...], 0, 0)
    bias_row = 0.25 * jnp.concatenate(bias_sum, 1)
    gate_row = jnp.concatenate(gate_sum, 1)
    aux = jnp.concatenate(
        [row[:, 128 * k : 128 * (k + 1)] for row in (bias_row, gate_row) for k in range(3)]
        + [jnp.zeros((2, 128), f32)],
        0,
    )

    def put_spread(ref):
        for i in range(12):
            col = 128 * (i // 2)
            ref[i // 3, UNITS * (i % 3) : UNITS * (i % 3 + 1), :] = spread_terms[i % 2][
                :, col : col + 128
            ].astype(ref.dtype)
        ref[0, CHUNK:, :] = aux.astype(ref.dtype)
        ref[1:, CHUNK:, :] = jnp.zeros((3, AUX, 128), ref.dtype)

    def put_merge(ref):
        for i in range(12):
            row = UNITS * (i % 4)
            col = 128 * (i // 4)
            ref[i // 3, UNITS * (i % 3) : UNITS * (i % 3 + 1), :] = merge_term[
                row : row + UNITS, col : col + 128
            ].astype(ref.dtype)
        ref[:, CHUNK:, :] = jnp.zeros((4, AUX, 128), ref.dtype)

    @pl.when(core[0] == 0)
    def _():
        put_spread(keep)
        put_merge(send)

    @pl.when(core[0] != 0)
    def _():
        put_merge(keep)
        put_spread(send)


def core_sum_kernel(place, keep, came, own, first, second, third):
    for mask, ref in enumerate((own, first, second, third)):
        chunk = place[0] ^ mask
        ref[...] = (keep[chunk] + came[chunk].astype(f32)).astype(ref.dtype)


def ring_sum_kernel(own, first, second, third, slots):
    total = own[...] + first[...].astype(f32) + (second[...].astype(f32) + third[...].astype(f32))
    slots[: CHUNK + AUX, :] = total.astype(bf16)


def slot_sum_kernel(slots, sums):
    total = slots[0].astype(f32)
    for k in range(1, slots.shape[0]):
        total = total + slots[k].astype(f32)
    sums[...] = jnp.broadcast_to(total.astype(bf16)[None], sums.shape)


def collect_kernel(place, own, first, second, third, half):
    for mask, ref in enumerate((own, first, second, third)):
        half[place[0] ^ mask] = ref[...]


def finish_kernel(core, gate, mine, other, spread, merge, bias, gate_out, *, grad_scale):
    def write(first, second):
        for i in range(12):
            rows = slice(UNITS * (i % 3), UNITS * (i % 3 + 1))
            col = 128 * (i // 2)
            row = UNITS * (i % 2)
            spread[row : row + UNITS, col : col + 128] = (
                first[i // 3, rows, :].astype(f32) * grad_scale
            )
            col = 128 * (i // 4)
            row = UNITS * (i % 4)
            merge[row : row + UNITS, col : col + 128] = (
                second[i // 3, rows, :].astype(f32) * grad_scale
            )
        aux = first[0, CHUNK:, :].astype(f32) * grad_scale
        gate_open = jax.nn.sigmoid(gate[...])
        slope = gate_open * (1.0 - gate_open)
        for k in range(3):
            at = slice(128 * k, 128 * (k + 1))
            bias[:, at] = aux[k : k + 1, :]
            gate_out[:, at] = aux[3 + k : 4 + k, :] * slope[:, at]

    @pl.when(core[0] == 0)
    def _():
        write(mine, other)

    @pl.when(core[0] != 0)
    def _():
        write(other, mine)


def shaped(shape, dtype):
    return jax.ShapeDtypeStruct(shape, dtype)


VMEM = pl.BlockSpec(memory_space=pltpu.VMEM)
SMEM = pl.BlockSpec(memory_space=pltpu.SMEM)


def call(kernel, outs, ins, scalars=0, scratch=(), name=None):
    return pl.pallas_call(
        kernel,
        out_shape=outs,
        in_specs=[SMEM] * scalars + [VMEM] * (len(ins) - scalars),
        out_specs=jax.tree.map(lambda _: VMEM, outs),
        scratch_shapes=list(scratch),
        name=name,
        compiler_params=pltpu.CompilerParams(vmem_limit_bytes=56 * 2**20),
    )(*ins)


def bit_groups(count, bits):
    mask = sum(1 << b for b in bits)
    groups = []
    for base in range(count):
        if base & mask:
            continue
        group = [base]
        for b in sorted(bits):
            group = group + [g | (1 << b) for g in group]
        groups.append(group)
    return groups


def exchange(value, mask):
    return lax.ppermute(value, "seq", [(i, i ^ mask) for i in range(lax.axis_size("seq"))])


def on_device(tokens, out_grad, spread_weight, merge_weight, switch_bias, gate_logit):
    count = lax.axis_size("seq")
    grad_scale = 1.0 / math.sqrt(count * tokens.shape[0])
    position = lax.axis_index("seq")
    core = (position % 2).astype(jnp.int32).reshape(1)
    place = (position // 2 % 4).astype(jnp.int32).reshape(1)
    members = bit_groups(count, (4, 5, 6, 7))
    planes = bit_groups(count, (3, 4, 5, 6, 7))

    def swap_rows(packed):
        return lax.all_to_all(packed, "seq", 0, 0, axis_index_groups=members)

    def swap_slots(slots):
        return lax.all_to_all(slots, "seq", 0, 0, axis_index_groups=planes)

    packed = jnp.concatenate([tokens, out_grad], 1).reshape(MEMBERS, ROWS, SWITCH)
    packed = swap_rows(packed)
    bias = switch_bias.reshape(1, SWITCH)
    gate = gate_logit.reshape(1, SWITCH)
    total = SECTIONS * PAIRS
    half = (4, CHUNK + AUX, 128)
    packed_out, send, keep = call(
        switch_kernel,
        (shaped((MEMBERS, ROWS, SWITCH), bf16), shaped(half, bf16), shaped(half, f32)),
        (core, packed, spread_weight, merge_weight, bias, gate),
        1,
        [
            pltpu.VMEM((MEMBERS, ROWS, UNITS), bf16),
            pltpu.VMEM((MEMBERS, ROWS, UNITS), bf16),
            pltpu.VMEM((total, UNITS), bf16),
            pltpu.VMEM((total, UNITS), bf16),
            pltpu.VMEM((PAIRS, HIDDEN), f32),
            pltpu.VMEM((total, HIDDEN), f32),
            pltpu.VMEM((total, HIDDEN), f32),
            pltpu.VMEM((total, HIDDEN), bf16),
            pltpu.VMEM((total, 128), f32),
            pltpu.VMEM((total, SWITCH), bf16),
            pltpu.VMEM((total, HIDDEN), bf16),
        ],
        name="switch",
    )
    came = exchange(send, 1)
    piece = (CHUNK + AUX, 128)
    own, *others = call(
        core_sum_kernel,
        (shaped(piece, f32),) + (shaped(piece, bf16),) * 3,
        (place, keep, came),
        1,
        name="core_sum",
    )
    others = [exchange(value, 2 * (k + 1)) for k, value in enumerate(others)]
    packed_out = swap_rows(packed_out)
    slots = call(
        ring_sum_kernel, shaped((32 * SLOT, 128), bf16), (own, *others), name="ring_sum"
    )
    slots = swap_slots(slots.reshape(32, SLOT, 128))
    sums = call(slot_sum_kernel, shaped(slots.shape, bf16), (slots,), name="slot_sum")
    sums = swap_slots(sums).reshape(32 * SLOT, 128)[: CHUNK + AUX]
    others = [exchange(sums, 2 * (k + 1)) for k in range(3)]
    mine = call(collect_kernel, shaped(half, bf16), (place, sums, *others), 1, name="collect")
    other = exchange(mine, 1)
    spread_grad, merge_grad, bias_grad, gate_grad = call(
        lambda *refs: finish_kernel(*refs, grad_scale=grad_scale),
        (
            shaped((SWITCH, HIDDEN), f32),
            shaped((HIDDEN, SWITCH), f32),
            shaped((1, SWITCH), f32),
            shaped((1, SWITCH), f32),
        ),
        (core, gate, mine, other),
        1,
        name="finish",
    )
    packed_out = packed_out.reshape(tokens.shape[0], SWITCH)
    return (
        packed_out[:, :UNITS],
        packed_out[:, UNITS:],
        spread_grad,
        merge_grad,
        bias_grad.reshape(SWITCH),
        gate_grad.reshape(SWITCH),
    )


def solution(mesh):
    placed = (P("seq", None), P("seq", None), P(), P(), P(), P())
    return jax.shard_map(
        on_device,
        mesh=mesh,
        in_specs=placed,
        out_specs=(P("seq", None), P("seq", None), P(), P(), P(), P()),
        check_vma=False,
    )
```

time: 424 us -> 133 us (0.31)
  waiting for transfers between devices: 199 us -> 33.6 us
  blocking collectives: 82.1 us -> 30.8 us
  matrix products: 33.6 us -> 0 us
  Pallas kernels: 0 us -> 33.4 us
  local copies, waits for them, and re-layouts: 38.6 us -> 7.55 us
  other arithmetic: 29.2 us -> 3.6 us
  between operations: 15.2 us -> 0.75 us
    psum x1 -> x0, waiting for transfers between devices: 181 us -> none  [on_device(): lax.psum((spread_total, merge_total, bias_total, gate_total), 'seq')]
    psum x1 -> x0, blocking collectives: 82.1 us -> none  [on_device(): lax.psum((spread_total, merge_total, bias_total, gate_total), 'seq')]
    dot_general x24 -> x0, matrix products: 33.6 us -> none  [the longest x4 9.99 us: switch_backward(): lax.dot_general(branch_grad, merge_weight, (((1,), (1,)), ((), ())), pref...]
    pallas_call x0 -> x6, Pallas kernels: none -> 33.4 us  [call(): pl.pallas_call(kernel, out_shape=outs, in_specs=[SMEM] * scalars + [VMEM]...]
    all_to_all x0 -> x2, blocking collectives: none -> 30.8 us  [swap_slots(): return lax.all_to_all(slots, 'seq', 0, 0, axis_index_groups=planes)]
    reshape x24 -> x2, local copies, waits for them, and re-layouts: 20.7 us -> 1.13 us  [the longest x1 0.56 us: on_device(): gate = gate_logit.reshape(1, SWITCH)]
    all_to_all x0 -> x2, waiting for transfers between devices: none -> 17.3 us  [swap_rows(): return lax.all_to_all(packed, 'seq', 0, 0, axis_index_groups=members)]
    all_to_all x0 -> x2, starting transfers between devices: none -> 14 us  [swap_rows(): return lax.all_to_all(packed, 'seq', 0, 0, axis_index_groups=members)]
  transfers between devices with their start and end apart: 9 -> 10, of which waited for: 5 -> 8; matrix products, arithmetic and copies ran while one was open for 10% -> 2% of each run, Pallas kernels for 0% -> 2%
where the time goes in v1:
time: 133 us
  waiting for transfers between devices  33.6 us (25%)
  Pallas kernels  33.4 us (25%)
  blocking collectives  30.8 us (23%)
  starting transfers between devices  23 us (17%)
  local copies, waits for them, and re-layouts  7.55 us (6%)
  other arithmetic  3.6 us (3%)
    pallas_call x6, Pallas kernels, call(): pl.pallas_call(kernel, out_shape=outs, in_specs=[SMEM] * scalars + [VMEM]...  33.4 us
    all_to_all x2, blocking collectives, swap_slots(): return lax.all_to_all(slots, 'seq', 0, 0, axis_index_groups=planes)  30.8 us
    all_to_all x2, waiting for transfers between devices, swap_rows(): return lax.all_to_all(packed, 'seq', 0, 0, axis_index_groups=members)  17.3 us
    ppermute x8, waiting for transfers between devices, exchange(): lax.ppermute(value, 'seq', [(i, i ^ mask) for i in range(lax.axis_size('s...  16.3 us
    all_to_all x2, starting transfers between devices, swap_rows(): return lax.all_to_all(packed, 'seq', 0, 0, axis_index_groups=members)  14 us
    ppermute x8, starting transfers between devices, exchange(): lax.ppermute(value, 'seq', [(i, i ^ mask) for i in range(lax.axis_size('s...  9.06 us
    unnamed x26, local copies, waits for them, and re-layouts  5.35 us
  transfers between devices with their start and end apart: 10, of which 8 were waited for; matrix products, arithmetic and copies ran while one was open for 2% of the time, Pallas kernels for 2%

profile of v1, /device:TPU:32, one launch (start us, length us, event | category | flops | bytes accessed | tf_op | source)
XLA Modules:
  0.0 132.7 jit_solution(15983953460877984877)
XLA Ops:
  0.7 1.1 pad_maximum_fusion
  1.7 0.9 copy.12
  2.6 10.3 %all-to-all-start = ((bf16[16,32,384]{2,1,0:T(8,128)(2,1)}), bf16[16,32,384]{2,1,0:T(8,128)(2,1)S(1)}, u32[]{:S(2)}, u32[]{:S(2)}) async-start(bf16[16,32,384]{2,1,0:T(8,128)(2,1)} %bitcast.1), calls=%async_computation | async-start | bytes 786432 | tf_op jit(solution)/shard_map/all_to_all | solution.py:291
  14.1 15.0 %all-to-all-done.packed = bf16[16,32,384]{2,1,0:T(8,128)(2,1)S(1)} async-done(((bf16[16,32,384]{2,1,0:T(8,128)(2,1)}), bf16[16,32,384]{2,1,0:T(8,128)(2,1)S(1)}, u32[]{:S(2)}, u32[]{:S(2)}) %all-to-all-start) | async-done | bytes 393248 | tf_op jit(solution)/shard_map/all_to_all | solution.py:291
  29.8 22.6 %switch.1 = (bf16[16,32,384]{2,1,0:T(8,128)(2,1)}, bf16[4,584,128]{2,1,0:T(8,128)(2,1)}, f32[4,584,128]{2,1,0:T(8,128)}) custom-call(s32[1]{0:T(128)} %bitcast.core.refs_0_, bf16[16,32,384]{2,1,0:T(8,128)(2,1)} %copy-done, bf16[384,768]{1,0:T(8,128)(2,1)} %spread.1, bf16[768,384]{1,0:T(8,128)(2,1)} %merge.1, f32[1,384]{1,0:T(1,128)} %reshape.44.bias, ...), custom_call_target="tpu_custom_call" | custom-call | tf_op jit(solution)/shard_map/switch/pallas_call | solution.py:253
  52.4 2.2 %collective-permute-done.came = bf16[4,584,128]{2,1,0:T(8,128)(2,1)S(1)} collective-permute-done((bf16[4,584,128]{2,1,0:T(8,128)(2,1)}, bf16[4,584,128]{2,1,0:T(8,128)(2,1)S(1)}, u32[]{:S(2)}, u32[]{:S(2)}) %collective-permute-start) | collective-permute-done | bytes 598048 | tf_op jit(solution)/shard_map/ppermute | solution.py:278
  55.5 2.4 %core_sum.1 = (f32[584,128]{1,0:T(8,128)}, bf16[584,128]{1,0:T(8,128)(2,1)}, bf16[584,128]{1,0:T(8,128)(2,1)}, bf16[584,128]{1,0:T(8,128)(2,1)}) custom-call(s32[1]{0:T(128)} %bitcast.3.place, f32[4,584,128]{2,1,0:T(8,128)} %get-tuple-element.18.keep, bf16[4,584,128]{2,1,0:T(8,128)(2,1)} %copy-done.3), custom_call_target="tpu_custom_call" | custom-call | tf_op jit(solution)/shard_map/core_sum/pallas_call | solution.py:253
  57.9 1.5 %collective-permute-start.1 = (bf16[584,128]{1,0:T(8,128)(2,1)}, bf16[584,128]{1,0:T(8,128)(2,1)S(1)}, u32[]{:S(2)}, u32[]{:S(2)}) collective-permute-start(bf16[584,128]{1,0:T(8,128)(2,1)} %get-tuple-element.21), channel_id=1, source_target_pairs={{0,2},{1,3},{2,0},{3,1},{4,6},{5,7},{6,4},{7,5},{8,10},{9,11},{10,... | collective-permute-start | bytes 448520 | tf_op jit(solution)/shard_map/ppermute | solution.py:278
  59.3 2.7 %collective-permute-start.2 = (bf16[584,128]{1,0:T(8,128)(2,1)}, bf16[584,128]{1,0:T(8,128)(2,1)S(1)}, u32[]{:S(2)}, u32[]{:S(2)}) collective-permute-start(bf16[584,128]{1,0:T(8,128)(2,1)} %get-tuple-element.22), channel_id=1, source_target_pairs={{0,4},{1,5},{2,6},{3,7},{4,0},{5,1},{6,2},{7,3},{8,12},{9,13},{10,... | collective-permute-start | bytes 448520 | tf_op jit(solution)/shard_map/ppermute | solution.py:278
  62.6 2.3 %collective-permute-done.1.first = bf16[584,128]{1,0:T(8,128)(2,1)S(1)} collective-permute-done((bf16[584,128]{1,0:T(8,128)(2,1)}, bf16[584,128]{1,0:T(8,128)(2,1)S(1)}, u32[]{:S(2)}, u32[]{:S(2)}) %collective-permute-start.1) | collective-permute-done | bytes 149536 | tf_op jit(solution)/shard_map/ppermute | solution.py:278
  64.8 4.7 %collective-permute-done.2.second = bf16[584,128]{1,0:T(8,128)(2,1)S(1)} collective-permute-done((bf16[584,128]{1,0:T(8,128)(2,1)}, bf16[584,128]{1,0:T(8,128)(2,1)S(1)}, u32[]{:S(2)}, u32[]{:S(2)}) %collective-permute-start.2) | collective-permute-done | bytes 149536 | tf_op jit(solution)/shard_map/ppermute | solution.py:278
  69.5 2.4 %collective-permute-done.3.third = bf16[584,128]{1,0:T(8,128)(2,1)S(1)} collective-permute-done((bf16[584,128]{1,0:T(8,128)(2,1)}, bf16[584,128]{1,0:T(8,128)(2,1)S(1)}, u32[]{:S(2)}, u32[]{:S(2)}) %collective-permute-start.3) | collective-permute-done | bytes 149536 | tf_op jit(solution)/shard_map/ppermute | solution.py:278
  72.6 1.9 %ring_sum.1 = bf16[768,128]{1,0:T(8,128)(2,1)} custom-call(f32[584,128]{1,0:T(8,128)} %get-tuple-element.20.own, bf16[584,128]{1,0:T(8,128)(2,1)} %copy-done.7, bf16[584,128]{1,0:T(8,128)(2,1)} %copy-done.8, bf16[584,128]{1,0:T(8,128)(2,1)} %copy-done.9), custom_call_target="tpu_custom_call" | custom-call | tf_op jit(solution)/shard_map/ring_sum/pallas_call | solution.py:253
  74.5 16.0 %all_to_all.20.slots = bf16[32,24,128]{2,1,0:T(8,128)(2,1)} all-to-all(bf16[32,24,128]{2,1,0:T(8,128)(2,1)} %bitcast.7), channel_id=1, replica_groups={{0,8,16,24,32,40,48,56,64,72,80,88,96,104,112,120,128,136,144,152,160,1..., dimensions={0} | all-to-all | bytes 393216 | tf_op jit(solution)/shard_map/all_to_all | solution.py:294
  90.5 1.7 %slot_sum.1 = bf16[32,24,128]{2,1,0:T(8,128)(2,1)} custom-call(bf16[32,24,128]{2,1,0:T(8,128)(2,1)} %all_to_all.20.slots), custom_call_target="tpu_custom_call" | custom-call | tf_op jit(solution)/shard_map/slot_sum/pallas_call | solution.py:253
  92.1 14.8 %all_to_all.21 = bf16[32,24,128]{2,1,0:T(8,128)(2,1)S(1)} all-to-all(bf16[32,24,128]{2,1,0:T(8,128)(2,1)} %slot_sum.1), channel_id=1, replica_groups={{0,8,16,24,32,40,48,56,64,72,80,88,96,104,112,120,128,136,144,152,160,1..., dimensions={0} | all-to-all | bytes 393216 | tf_op jit(solution)/shard_map/all_to_all | solution.py:294
  106.9 3.7 %all-to-all-start.1 = ((bf16[16,32,384]{2,1,0:T(8,128)(2,1)}), bf16[16,32,384]{2,1,0:T(8,128)(2,1)S(1)}, u32[]{:S(2)}, u32[]{:S(2)}) async-start(bf16[16,32,384]{2,1,0:T(8,128)(2,1)} %get-tuple-element.17), calls=%async_computation.1 | async-start | bytes 786432 | tf_op jit(solution)/shard_map/all_to_all | solution.py:291
  111.7 3.3 %collective-permute-start.4 = (bf16[584,128]{1,0:T(8,128)(2,1)S(1)}, bf16[584,128]{1,0:T(8,128)(2,1)S(1)}, u32[]{:S(2)}, u32[]{:S(2)}) collective-permute-start(bf16[584,128]{1,0:T(8,128)(2,1)S(1)} %slice.14.own), channel_id=1, source_target_pairs={{0,2},{1,3},{2,0},{3,1},{4,6},{5,7},{6,4},{7,5},{8,10},{9,11},{10,... | collective-permute-start | bytes 448520 | tf_op jit(solution)/shard_map/ppermute | solution.py:278
  115.0 3.9 %collective-permute-done.6.third = bf16[584,128]{1,0:T(8,128)(2,1)S(1)} collective-permute-done((bf16[584,128]{1,0:T(8,128)(2,1)S(1)}, bf16[584,128]{1,0:T(8,128)(2,1)S(1)}, u32[]{:S(2)}, u32[]{:S(2)}) %collective-permute-start.6) | collective-permute-done | bytes 149536 | tf_op jit(solution)/shard_map/ppermute | solution.py:278
  120.4 2.0 %collect.1.refs_2_ = bf16[4,584,128]{2,1,0:T(8,128)(2,1)} custom-call(s32[1]{0:T(128)} %bitcast.3.place, bf16[584,128]{1,0:T(8,128)(2,1)} %copy-done.1, bf16[584,128]{1,0:T(8,128)(2,1)} %copy-done.6, bf16[584,128]{1,0:T(8,128)(2,1)} %copy-done.5, bf16[584,128]{1,0:T(8,128)(2,1)} %copy-done.4), custom_call_target="tpu_custom_call" | custom-call | tf_op jit(solution)/shard_map/collect/pallas_call | solution.py:253
  122.4 2.3 %all-to-all-done.1 = bf16[16,32,384]{2,1,0:T(8,128)(2,1)S(1)} async-done(((bf16[16,32,384]{2,1,0:T(8,128)(2,1)}), bf16[16,32,384]{2,1,0:T(8,128)(2,1)S(1)}, u32[]{:S(2)}, u32[]{:S(2)}) %all-to-all-start.1) | async-done | bytes 393248 | tf_op jit(solution)/shard_map/all_to_all | solution.py:291
  127.3 2.9 %finish.1 = (f32[384,768]{1,0:T(8,128)}, f32[768,384]{1,0:T(8,128)}, f32[1,384]{1,0:T(1,128)}, f32[1,384]{1,0:T(1,128)}) custom-call(s32[1]{0:T(128)} %bitcast.core.refs_0_, f32[1,384]{1,0:T(1,128)} %reshape.45.gate.refs_1_, bf16[4,584,128]{2,1,0:T(8,128)(2,1)} %collect.1.refs_2_, bf16[4,584,128]{2,1,0:T(8,128)(2,1)} %copy-done.2), custom_call_target="tpu_custom_call" | custom-call | tf_op jit(solution)/shard_map/finish/pallas_call | solution.py:253
  130.2 1.3 reduce
  131.5 1.3 reduce.1
  (38 shorter events, 9.0 us)
Async XLA Ops:
  0.6 12.3 %copy-start.10 = (f32[384]{0:T(512)S(1)}, f32[384]{0:T(512)}, u32[]{:S(2)}) copy-start(f32[384]{0:T(512)} %param.11) | copy-start | bytes 4612
  0.6 12.9 %copy-start.11 = (f32[384]{0:T(512)S(1)}, f32[384]{0:T(512)}, u32[]{:S(2)}) copy-start(f32[384]{0:T(512)} %param.10) | copy-start | bytes 4612
  2.6 26.5 %all-to-all-start = ((bf16[16,32,384]{2,1,0:T(8,128)(2,1)}), bf16[16,32,384]{2,1,0:T(8,128)(2,1)S(1)}, u32[]{:S(2)}, u32[]{:S(2)}) async-start(bf16[16,32,384]{2,1,0:T(8,128)(2,1)} %bitcast.1), calls=%async_computation | async-start | bytes 786432 | tf_op jit(solution)/shard_map/all_to_all | solution.py:291
  29.1 0.7 copy-start
  52.4 2.2 %collective-permute-start = (bf16[4,584,128]{2,1,0:T(8,128)(2,1)}, bf16[4,584,128]{2,1,0:T(8,128)(2,1)S(1)}, u32[]{:S(2)}, u32[]{:S(2)}) collective-permute-start(bf16[4,584,128]{2,1,0:T(8,128)(2,1)} %get-tuple-element.19), channel_id=1, source_target_pairs={{0,1},{1,0},{2,3},{3,2},{4,5},{5,4},{6,7},{7,6},{8,9},{9,8},{10,11... | collective-permute-start | bytes 1794056 | tf_op jit(solution)/shard_map/ppermute | solution.py:278
  54.6 0.8 copy-start.3
  57.9 7.0 %collective-permute-start.1 = (bf16[584,128]{1,0:T(8,128)(2,1)}, bf16[584,128]{1,0:T(8,128)(2,1)S(1)}, u32[]{:S(2)}, u32[]{:S(2)}) collective-permute-start(bf16[584,128]{1,0:T(8,128)(2,1)} %get-tuple-element.21), channel_id=1, source_target_pairs={{0,2},{1,3},{2,0},{3,1},{4,6},{5,7},{6,4},{7,5},{8,10},{9,11},{10,... | collective-permute-start | bytes 448520 | tf_op jit(solution)/shard_map/ppermute | solution.py:278
  59.3 10.2 %collective-permute-start.2 = (bf16[584,128]{1,0:T(8,128)(2,1)}, bf16[584,128]{1,0:T(8,128)(2,1)S(1)}, u32[]{:S(2)}, u32[]{:S(2)}) collective-permute-start(bf16[584,128]{1,0:T(8,128)(2,1)} %get-tuple-element.22), channel_id=1, source_target_pairs={{0,4},{1,5},{2,6},{3,7},{4,0},{5,1},{6,2},{7,3},{8,12},{9,13},{10,... | collective-permute-start | bytes 448520 | tf_op jit(solution)/shard_map/ppermute | solution.py:278
  62.1 9.8 %collective-permute-start.3 = (bf16[584,128]{1,0:T(8,128)(2,1)}, bf16[584,128]{1,0:T(8,128)(2,1)S(1)}, u32[]{:S(2)}, u32[]{:S(2)}) collective-permute-start(bf16[584,128]{1,0:T(8,128)(2,1)} %get-tuple-element.23), channel_id=1, source_target_pairs={{0,6},{1,7},{2,4},{3,5},{4,2},{5,3},{6,0},{7,1},{8,14},{9,15},{10,... | collective-permute-start | bytes 448520 | tf_op jit(solution)/shard_map/ppermute | solution.py:278
  64.8 7.1 %copy-start.7 = (bf16[584,128]{1,0:T(8,128)(2,1)}, bf16[584,128]{1,0:T(8,128)(2,1)S(1)}, u32[]{:S(2)}) copy-start(bf16[584,128]{1,0:T(8,128)(2,1)S(1)} %collective-permute-done.1.first) | copy-start | bytes 448516
  69.5 2.4 %copy-start.8 = (bf16[584,128]{1,0:T(8,128)(2,1)}, bf16[584,128]{1,0:T(8,128)(2,1)S(1)}, u32[]{:S(2)}) copy-start(bf16[584,128]{1,0:T(8,128)(2,1)S(1)} %collective-permute-done.2.second) | copy-start | bytes 448516
  71.9 0.7 copy-start.9
  106.9 17.8 %all-to-all-start.1 = ((bf16[16,32,384]{2,1,0:T(8,128)(2,1)}), bf16[16,32,384]{2,1,0:T(8,128)(2,1)S(1)}, u32[]{:S(2)}, u32[]{:S(2)}) async-start(bf16[16,32,384]{2,1,0:T(8,128)(2,1)} %get-tuple-element.17), calls=%async_computation.1 | async-start | bytes 786432 | tf_op jit(solution)/shard_map/all_to_all | solution.py:291
  110.6 9.1 %copy-start.1 = (bf16[584,128]{1,0:T(8,128)(2,1)}, bf16[584,128]{1,0:T(8,128)(2,1)S(1)}, u32[]{:S(2)}) copy-start(bf16[584,128]{1,0:T(8,128)(2,1)S(1)} %slice.14.own) | copy-start | bytes 448516
  110.6 8.3 %collective-permute-start.6 = (bf16[584,128]{1,0:T(8,128)(2,1)S(1)}, bf16[584,128]{1,0:T(8,128)(2,1)S(1)}, u32[]{:S(2)}, u32[]{:S(2)}) collective-permute-start(bf16[584,128]{1,0:T(8,128)(2,1)S(1)} %slice.14.own), channel_id=1, source_target_pairs={{0,6},{1,7},{2,4},{3,5},{4,2},{5,3},{6,0},{7,1},{8,14},{9,15},{10,... | collective-permute-start | bytes 448520 | tf_op jit(solution)/shard_map/ppermute | solution.py:278
  111.4 7.5 %collective-permute-start.5 = (bf16[584,128]{1,0:T(8,128)(2,1)S(1)}, bf16[584,128]{1,0:T(8,128)(2,1)S(1)}, u32[]{:S(2)}, u32[]{:S(2)}) collective-permute-start(bf16[584,128]{1,0:T(8,128)(2,1)S(1)} %slice.14.own), channel_id=1, source_target_pairs={{0,4},{1,5},{2,6},{3,7},{4,0},{5,1},{6,2},{7,3},{8,12},{9,13},{10,... | collective-permute-start | bytes 448520 | tf_op jit(solution)/shard_map/ppermute | solution.py:278
  111.7 8.0 %collective-permute-start.4 = (bf16[584,128]{1,0:T(8,128)(2,1)S(1)}, bf16[584,128]{1,0:T(8,128)(2,1)S(1)}, u32[]{:S(2)}, u32[]{:S(2)}) collective-permute-start(bf16[584,128]{1,0:T(8,128)(2,1)S(1)} %slice.14.own), channel_id=1, source_target_pairs={{0,2},{1,3},{2,0},{3,1},{4,6},{5,7},{6,4},{7,5},{8,10},{9,11},{10,... | collective-permute-start | bytes 448520 | tf_op jit(solution)/shard_map/ppermute | solution.py:278
  118.9 0.8 copy-start.4
  118.9 0.8 copy-start.5
  119.8 0.7 copy-start.6
  122.4 4.1 %collective-permute-start.7 = (bf16[4,584,128]{2,1,0:T(8,128)(2,1)}, bf16[4,584,128]{2,1,0:T(8,128)(2,1)S(1)}, u32[]{:S(2)}, u32[]{:S(2)}) collective-permute-start(bf16[4,584,128]{2,1,0:T(8,128)(2,1)} %collect.1.refs_2_), channel_id=1, source_target_pairs={{0,1},{1,0},{2,3},{3,2},{4,5},{5,4},{6,7},{7,6},{8,9},{9,8},{10,11... | collective-permute-start | bytes 1794056 | tf_op jit(solution)/shard_map/ppermute | solution.py:278
  126.5 0.8 copy-start.2

commit v2 on v1

v2 whole, which is shorter than its diff:
```python
import math

import jax
import jax.numpy as jnp
from jax import lax
from jax.experimental import pallas as pl
from jax.experimental.pallas import tpu as pltpu
from jax.sharding import PartitionSpec as P


SECTIONS = 4
MEMBERS = 16
ROWS = 32
UNITS = 192
SWITCH = 384
HIDDEN = 768
PAIRS = 256
CHUNK = 576
AUX = 8
SLOT = 24
BLOCK = 32
ORDER = [4 * i % MEMBERS + i // 4 for i in range(MEMBERS)]

sqrt_half = 0.7071067811865476
inv_sqrt_two_pi = 0.3989422804014327
f32 = jnp.float32
bf16 = jnp.bfloat16


def dot(a, b, ca, cb):
    return lax.dot_general(a, b, (((ca,), (cb,)), ((), ())), preferred_element_type=f32)


def sides(section):
    bit = MEMBERS >> (section + 1)
    lower = [g for g in range(MEMBERS) if not g & bit]
    return lower, [g + bit for g in lower]


def load_rows(ref, members):
    return jnp.concatenate([ref[g] for g in members], 0)


def store_rows(ref, members, value):
    for k, g in enumerate(members):
        ref[g] = value[ROWS * k : ROWS * (k + 1)]


def add_to(ref, section, term):
    if section == SECTIONS - 1:
        ref[...] = term
    else:
        ref[...] += term


def switch_kernel(
    core,
    packed,
    spread,
    merge,
    bias,
    gate,
    packed_out,
    send,
    keep,
    state,
    grad,
    left,
    right,
    pre,
    normed,
    slope,
    hidden,
    scale,
    dbranch,
    dpre,
    spread_sum,
    merge_sum,
):
    gate_open = jax.nn.sigmoid(gate[...])
    gate_left = gate_open[:, :UNITS]
    gate_right = gate_open[:, UNITS:]
    bias_left = 0.25 * bias[:, :UNITS]
    bias_right = 0.25 * bias[:, UNITS:]
    for i, g in enumerate(ORDER):
        state[g] = packed[i, :, :UNITS]
        grad[g] = packed[i, :, UNITS:]
    for section in range(SECTIONS):
        lower, upper = sides(section)
        base = PAIRS * section
        rows = slice(base, base + PAIRS)
        x_left = load_rows(state, lower)
        x_right = load_rows(state, upper)
        left[rows] = x_left
        right[rows] = x_right
        pre[...] = dot(x_left, spread[:UNITS, :], 1, 0) + dot(x_right, spread[UNITS:, :], 1, 0)

        def forward(block, carry, base=base):
            start = pl.multiple_of(block * BLOCK, BLOCK)
            at = pl.ds(start, BLOCK)
            to = pl.ds(base + start, BLOCK)
            value = pre[at, :]
            centered = value - jnp.mean(value, -1, keepdims=True)
            inv = lax.rsqrt(jnp.mean(centered * centered, -1, keepdims=True) + 1e-05)
            norm = centered * inv
            cdf = 0.5 * (1.0 + lax.erf(norm * sqrt_half))
            normed[to, :] = norm
            slope[to, :] = cdf + norm * jnp.exp(-0.5 * norm * norm) * inv_sqrt_two_pi
            hidden[to, :] = (norm * cdf).astype(bf16)
            scale[to, :] = jnp.broadcast_to(inv, (BLOCK, 128))
            return carry

        lax.fori_loop(0, PAIRS // BLOCK, forward, 0, unroll=PAIRS // BLOCK)
        act = hidden[rows, :]
        branch_left = dot(act, merge[:, :UNITS], 1, 0)
        branch_right = dot(act, merge[:, UNITS:], 1, 0)
        out_left = gate_left * x_left.astype(f32) + (0.25 * branch_left + bias_left)
        out_right = gate_right * x_right.astype(f32) + (0.25 * branch_right + bias_right)
        store_rows(state, lower, out_left.astype(bf16))
        store_rows(state, upper, out_right.astype(bf16))
    for i, g in enumerate(ORDER):
        packed_out[i, :, :UNITS] = state[g]

    bias_sum = [jnp.zeros((1, UNITS), f32)] * 2
    gate_sum = [jnp.zeros((1, UNITS), f32)] * 2
    for section in reversed(range(SECTIONS)):
        lower, upper = sides(section)
        base = PAIRS * section
        rows = slice(base, base + PAIRS)
        d_left = load_rows(grad, lower)
        d_right = load_rows(grad, upper)
        wide_left = d_left.astype(f32)
        wide_right = d_right.astype(f32)
        bias_sum[0] += jnp.sum(wide_left, 0, keepdims=True)
        bias_sum[1] += jnp.sum(wide_right, 0, keepdims=True)
        gate_sum[0] += jnp.sum(wide_left * left[rows].astype(f32), 0, keepdims=True)
        gate_sum[1] += jnp.sum(wide_right * right[rows].astype(f32), 0, keepdims=True)
        b_left = (0.25 * wide_left).astype(bf16)
        b_right = (0.25 * wide_right).astype(bf16)
        dbranch[rows, :UNITS] = b_left
        dbranch[rows, UNITS:] = b_right
        pre[...] = dot(b_left, merge[:, :UNITS], 1, 1) + dot(b_right, merge[:, UNITS:], 1, 1)
        add_to(merge_sum, section, dot(hidden[rows, :], dbranch[rows, :], 0, 0))

        def backward(block, carry, base=base):
            start = pl.multiple_of(block * BLOCK, BLOCK)
            at = pl.ds(start, BLOCK)
            to = pl.ds(base + start, BLOCK)
            norm = normed[to, :]
            dn = pre[at, :] * slope[to, :]
            mean = jnp.mean(dn, -1, keepdims=True)
            along = jnp.mean(dn * norm, -1, keepdims=True)
            inv = scale[to, :][:, :1]
            dpre[to, :] = (inv * (dn - mean - norm * along)).astype(bf16)
            return carry

        lax.fori_loop(0, PAIRS // BLOCK, backward, 0, unroll=PAIRS // BLOCK)
        back = dpre[rows, :]
        g_left = gate_left * wide_left + dot(back, spread[:UNITS, :], 1, 1)
        g_right = gate_right * wide_right + dot(back, spread[UNITS:, :], 1, 1)
        store_rows(grad, lower, g_left.astype(bf16))
        store_rows(grad, upper, g_right.astype(bf16))
        add_to(spread_sum.at[:UNITS], section, dot(left[rows], back, 0, 0))
        add_to(spread_sum.at[UNITS:], section, dot(right[rows], back, 0, 0))
    for i, g in enumerate(ORDER):
        packed_out[i, :, UNITS:] = grad[g]

    bias_row = 0.25 * jnp.concatenate(bias_sum, 1)
    gate_row = jnp.concatenate(gate_sum, 1)
    aux = jnp.concatenate(
        [row[:, 128 * k : 128 * (k + 1)] for row in (bias_row, gate_row) for k in range(3)]
        + [jnp.zeros((2, 128), f32)],
        0,
    )

    def put_spread(ref):
        for q in range(4):
            for c in range(6):
                ref[q, 96 * c : 96 * (c + 1), :] = spread_sum[
                    96 * q : 96 * (q + 1), 128 * c : 128 * (c + 1)
                ].astype(ref.dtype)
        ref[0, CHUNK:, :] = aux.astype(ref.dtype)
        ref[1:, CHUNK:, :] = jnp.zeros((3, AUX, 128), ref.dtype)

    def put_merge(ref):
        for q in range(4):
            for c in range(3):
                ref[q, 192 * c : 192 * (c + 1), :] = merge_sum[
                    192 * q : 192 * (q + 1), 128 * c : 128 * (c + 1)
                ].astype(ref.dtype)
        ref[:, CHUNK:, :] = jnp.zeros((4, AUX, 128), ref.dtype)

    @pl.when(core[0] == 0)
    def _():
        put_spread(keep)
        put_merge(send)

    @pl.when(core[0] != 0)
    def _():
        put_merge(keep)
        put_spread(send)


def pack_kernel(tokens, out_grad, packed):
    rows = jnp.concatenate([tokens[...], out_grad[...]], 0).T
    for i, g in enumerate(ORDER):
        packed[i] = rows[ROWS * g : ROWS * (g + 1)]


def unpack_kernel(packed, network_out, token_grad):
    places = [ORDER.index(g) for g in range(MEMBERS)]
    columns = jnp.concatenate([packed[i] for i in places], 0).T
    network_out[...] = columns[:UNITS]
    token_grad[...] = columns[UNITS:]


def core_sum_kernel(place, keep, came, own, first, second, third):
    for mask, ref in enumerate((own, first, second, third)):
        chunk = place[0] ^ mask
        ref[...] = (keep[chunk] + came[chunk].astype(f32)).astype(ref.dtype)


def ring_sum_kernel(own, first, second, third, slots):
    total = own[...] + first[...].astype(f32) + (second[...].astype(f32) + third[...].astype(f32))
    slots[: CHUNK + AUX, :] = total.astype(bf16)
    slots[CHUNK + AUX :, :] = jnp.zeros((32 * SLOT - CHUNK - AUX, 128), bf16)


def slot_sum_kernel(slots, sums):
    total = slots[0].astype(f32)
    for k in range(1, slots.shape[0]):
        total = total + slots[k].astype(f32)
    sums[...] = jnp.broadcast_to(total.astype(bf16)[None], sums.shape)


def finish_kernel(core, place, gate, *refs, grad_scale):
    mine, theirs = refs[:4], refs[4:8]
    spread, merge, bias, gate_out = refs[8:]

    def write(firsts, seconds):
        for mask in range(4):
            chunk = place[0] ^ mask
            rows = pl.ds(pl.multiple_of(96 * chunk, 96), 96)
            for c in range(6):
                spread[rows, 128 * c : 128 * (c + 1)] = (
                    firsts[mask][96 * c : 96 * (c + 1), :].astype(f32) * grad_scale
                )
            rows = pl.ds(pl.multiple_of(192 * chunk, 192), 192)
            for c in range(3):
                merge[rows, 128 * c : 128 * (c + 1)] = (
                    seconds[mask][192 * c : 192 * (c + 1), :].astype(f32) * grad_scale
                )

            @pl.when(chunk == 0)
            def _(mask=mask):
                aux = firsts[mask][CHUNK:, :].astype(f32) * grad_scale
                gate_open = jax.nn.sigmoid(gate[...])
                slope = gate_open * (1.0 - gate_open)
                for k in range(3):
                    at = slice(128 * k, 128 * (k + 1))
                    bias[at] = aux[k, :]
                    gate_out[at] = aux[3 + k, :] * slope[0, at]

    @pl.when(core[0] == 0)
    def _():
        write(mine, theirs)

    @pl.when(core[0] != 0)
    def _():
        write(theirs, mine)


def shaped(shape, dtype):
    return jax.ShapeDtypeStruct(shape, dtype)


def near(shape, dtype):
    return pltpu.VMEM(shape, dtype)


VMEM = pl.BlockSpec(memory_space=pltpu.VMEM)
SMEM = pl.BlockSpec(memory_space=pltpu.SMEM)


def call(kernel, outs, ins, scalars=0, scratch=(), far=False):
    arrays = ins[scalars:]
    space = pltpu.HBM if far else pltpu.VMEM
    arrays = [pltpu.with_memory_space_constraint(a, space) for a in arrays]
    return pl.pallas_call(
        kernel,
        out_shape=outs,
        in_specs=[SMEM] * scalars + [VMEM] * len(arrays),
        out_specs=tuple(VMEM for _ in outs) if isinstance(outs, tuple) else VMEM,
        scratch_shapes=list(scratch),
        compiler_params=pltpu.CompilerParams(vmem_limit_bytes=40 * 2**20),
    )(*ins[:scalars], *arrays)


def bit_groups(count, bits):
    stride = 2 ** (len(bits) - 2)
    mask = sum(1 << b for b in bits)
    groups = []
    for base in range(count):
        if base & mask:
            continue
        group = [base]
        for b in sorted(bits):
            group = group + [g | (1 << b) for g in group]
        groups.append([group[stride * i % len(group) + i // 4] for i in range(len(group))])
    return groups


def exchange(value, mask):
    return lax.ppermute(value, "seq", [(i, i ^ mask) for i in range(lax.axis_size("seq"))])


def step(tokens, out_grad, spread_weight, merge_weight, switch_bias, gate_logit):
    count = lax.axis_size("seq")
    grad_scale = 1.0 / math.sqrt(count * tokens.shape[0])
    position = lax.axis_index("seq")
    core = (position % 2).astype(jnp.int32).reshape(1)
    place = (position // 2 % 4).astype(jnp.int32).reshape(1)
    members = bit_groups(count, (4, 5, 6, 7))
    planes = bit_groups(count, (3, 4, 5, 6, 7))

    def swap_rows(packed):
        return lax.all_to_all(packed, "seq", 0, 0, axis_index_groups=members)

    def swap_slots(slots):
        return lax.all_to_all(slots, "seq", 0, 0, axis_index_groups=planes)

    rows = tokens.shape[0]
    packed = call(
        pack_kernel, near((MEMBERS, ROWS, SWITCH), bf16), (tokens.T, out_grad.T), far=True
    )
    packed = swap_rows(packed)
    bias = switch_bias.reshape(1, SWITCH)
    gate = gate_logit.reshape(1, SWITCH)
    total = SECTIONS * PAIRS
    half = (4, CHUNK + AUX, 128)
    packed_out, send, keep = call(
        switch_kernel,
        (near((MEMBERS, ROWS, SWITCH), bf16), near(half, bf16), near(half, f32)),
        (core, packed, spread_weight, merge_weight, bias, gate),
        1,
        [
            pltpu.VMEM((MEMBERS, ROWS, UNITS), bf16),
            pltpu.VMEM((MEMBERS, ROWS, UNITS), bf16),
            pltpu.VMEM((total, UNITS), bf16),
            pltpu.VMEM((total, UNITS), bf16),
            pltpu.VMEM((PAIRS, HIDDEN), f32),
            pltpu.VMEM((total, HIDDEN), f32),
            pltpu.VMEM((total, HIDDEN), f32),
            pltpu.VMEM((total, HIDDEN), bf16),
            pltpu.VMEM((total, 128), f32),
            pltpu.VMEM((total, SWITCH), bf16),
            pltpu.VMEM((total, HIDDEN), bf16),
            pltpu.VMEM((SWITCH, HIDDEN), f32),
            pltpu.VMEM((HIDDEN, SWITCH), f32),
        ],
    )
    came = exchange(send, 1)
    piece = (CHUNK + AUX, 128)
    own, *others = call(
        core_sum_kernel, (near(piece, f32),) + (near(piece, bf16),) * 3, (place, keep, came), 1
    )
    others = [exchange(value, 2 * (k + 1)) for k, value in enumerate(others)]
    packed_out = swap_rows(packed_out)
    slots = call(ring_sum_kernel, near((32 * SLOT, 128), bf16), (own, *others))
    slots = swap_slots(slots.reshape(32, SLOT, 128))
    sums = call(slot_sum_kernel, near(slots.shape, bf16), (slots,))
    sums = swap_slots(sums)
    sums = sums.reshape(32 * SLOT, 128)[: CHUNK + AUX]
    mine = [sums]
    mine += [exchange(sums, 2 * (k + 1)) for k in range(3)]
    theirs = [exchange(value, 1) for value in mine]
    network_out, token_grad = call(unpack_kernel, (shaped((UNITS, rows), bf16),) * 2, (packed_out,))
    spread_grad, merge_grad, bias_grad, gate_grad = call(
        lambda *refs: finish_kernel(*refs, grad_scale=grad_scale),
        (
            shaped((SWITCH, HIDDEN), f32),
            shaped((HIDDEN, SWITCH), f32),
            shaped((SWITCH,), f32),
            shaped((SWITCH,), f32),
        ),
        (core, place, gate, *mine, *theirs),
        2,
    )
    return (network_out.T, token_grad.T, spread_grad, merge_grad, bias_grad, gate_grad)


def solution(mesh):
    placed = (P("seq", None), P("seq", None), P(), P(), P(), P())
    return jax.shard_map(
        step,
        mesh=mesh,
        in_specs=placed,
        out_specs=(P("seq", None), P("seq", None), P(), P(), P(), P()),
        check_vma=False,
    )
```

time: 133 us -> 104 us (0.78)
  Pallas kernels: 33.4 us -> 14.8 us
  local copies, waits for them, and re-layouts: 7.55 us -> 0.04 us
  other arithmetic: 3.6 us -> 0 us
    pallas_call x6 -> x7, Pallas kernels: 33.4 us -> 14.8 us  [call(): pl.pallas_call(kernel, out_shape=outs, in_specs=[SMEM] * scalars + [VMEM]...]
    unnamed x26 -> x8, local copies, waits for them, and re-layouts: 5.35 us -> 0.02 us
    pallas_call x2 -> x0, other arithmetic: 2.54 us -> none  [call(): pl.pallas_call(kernel, out_shape=outs, in_specs=[SMEM] * scalars + [VMEM]...]
    ppermute x8 -> x11, waiting for transfers between devices: 16.3 us -> 15.4 us  [exchange(): lax.ppermute(value, 'seq', [(i, i ^ mask) for i in range(lax.axis_size('s...]
    ppermute x8 -> x11, starting transfers between devices: 9.06 us -> 9.48 us  [exchange(): lax.ppermute(value, 'seq', [(i, i ^ mask) for i in range(lax.axis_size('s...]
  transfers between devices with their start and end apart: 10 -> 13, of which waited for: 8 -> 8; matrix products, arithmetic and copies ran while one was open for 2% -> 0% of each run, Pallas kernels for 2% -> 1%
where the time goes in v2:
time: 104 us; the launch traced here: 103 us
  waiting for transfers between devices  33.3 us (32%)
  blocking collectives  30.6 us (29%)
  starting transfers between devices  23.5 us (23%)
  Pallas kernels  14.8 us (14%)
    all_to_all x2, blocking collectives, swap_slots(): return lax.all_to_all(slots, 'seq', 0, 0, axis_index_groups=planes)  30.6 us
    all_to_all x2, waiting for transfers between devices, swap_rows(): return lax.all_to_all(packed, 'seq', 0, 0, axis_index_groups=members)  17.9 us
    ppermute x11, waiting for transfers between devices, exchange(): lax.ppermute(value, 'seq', [(i, i ^ mask) for i in range(lax.axis_size('s...  15.4 us
    pallas_call x7, Pallas kernels, call(): pl.pallas_call(kernel, out_shape=outs, in_specs=[SMEM] * scalars + [VMEM]...  14.8 us
    all_to_all x2, starting transfers between devices, swap_rows(): return lax.all_to_all(packed, 'seq', 0, 0, axis_index_groups=members)  14.1 us
    ppermute x11, starting transfers between devices, exchange(): lax.ppermute(value, 'seq', [(i, i ^ mask) for i in range(lax.axis_size('s...  9.48 us
  transfers between devices with their start and end apart: 13, of which 8 were waited for; matrix products, arithmetic and copies ran while one was open for 0% of the time, Pallas kernels for 1%

profile of v2, /device:TPU:32, one launch (start us, length us, event | category | flops | bytes accessed | tf_op | source)
XLA Modules:
  0.0 103.1 jit_solution(11086732150849570462)
XLA Ops:
  0.7 2.0 %shard_map.109 = bf16[16,32,384]{2,1,0:T(8,128)(2,1)} custom-call(bf16[192,512]{1,0:T(8,128)(2,1)} %bitcast.10, bf16[192,512]{1,0:T(8,128)(2,1)} %bitcast.11), custom_call_target="tpu_custom_call" | custom-call | tf_op jit(solution)/shard_map/pallas_call | solution.py:289
  2.7 10.3 %all-to-all-start = ((bf16[16,32,384]{2,1,0:T(8,128)(2,1)}), bf16[16,32,384]{2,1,0:T(8,128)(2,1)S(1)}, u32[]{:S(2)}, u32[]{:S(2)}) async-start(bf16[16,32,384]{2,1,0:T(8,128)(2,1)} %shard_map.109), calls=%async_computation | async-start | bytes 786432 | tf_op jit(solution)/shard_map/all_to_all | solution.py:327
  13.1 14.7 %all-to-all-done.packed = bf16[16,32,384]{2,1,0:T(8,128)(2,1)S(1)} async-done(((bf16[16,32,384]{2,1,0:T(8,128)(2,1)}), bf16[16,32,384]{2,1,0:T(8,128)(2,1)S(1)}, u32[]{:S(2)}, u32[]{:S(2)}) %all-to-all-start) | async-done | bytes 393248 | tf_op jit(solution)/shard_map/all_to_all | solution.py:327
  27.7 10.0 %shard_map.110 = (bf16[16,32,384]{2,1,0:T(8,128)(2,1)}, bf16[4,584,128]{2,1,0:T(8,128)(2,1)S(1)}, f32[4,584,128]{2,1,0:T(8,128)S(1)}) custom-call(s32[1]{0:T(128)} %bitcast.core.refs_0_, bf16[16,32,384]{2,1,0:T(8,128)(2,1)S(1)} %all-to-all-done.packed, bf16[384,768]{1,0:T(8,128)(2,1)S(1)} %copy-done, bf16[768,384]{1,0:T(8,128)(2,1)S(1)} %copy-done.1, ...), custom_call_target="tpu_custom_call" | custom-call | tf_op jit(solution)/shard_map/pallas_call | solution.py:289
  37.7 2.0 %collective-permute-done.came = bf16[4,584,128]{2,1,0:T(8,128)(2,1)S(1)} collective-permute-done((bf16[4,584,128]{2,1,0:T(8,128)(2,1)S(1)}, bf16[4,584,128]{2,1,0:T(8,128)(2,1)S(1)}, u32[]{:S(2)}, u32[]{:S(2)}) %collective-permute-start) | collective-permute-done | bytes 598048 | tf_op jit(solution)/shard_map/ppermute | solution.py:314
  39.7 0.1 shard_map.112
  39.9 1.6 %collective-permute-start.1 = (bf16[584,128]{1,0:T(8,128)(2,1)S(1)}, bf16[584,128]{1,0:T(8,128)(2,1)S(1)}, u32[]{:S(2)}, u32[]{:S(2)}) collective-permute-start(bf16[584,128]{1,0:T(8,128)(2,1)S(1)} %get-tuple-element.25), channel_id=1, source_target_pairs={{0,2},{1,3},{2,0},{3,1},{4,6},{5,7},{6,4},{7,5},{8,10},{9,11},{10,... | collective-permute-start | bytes 448520 | tf_op jit(solution)/shard_map/ppermute | solution.py:314
  41.4 2.7 %collective-permute-start.2 = (bf16[584,128]{1,0:T(8,128)(2,1)S(1)}, bf16[584,128]{1,0:T(8,128)(2,1)S(1)}, u32[]{:S(2)}, u32[]{:S(2)}) collective-permute-start(bf16[584,128]{1,0:T(8,128)(2,1)S(1)} %get-tuple-element.26), channel_id=1, source_target_pairs={{0,4},{1,5},{2,6},{3,7},{4,0},{5,1},{6,2},{7,3},{8,12},{9,13},{10,... | collective-permute-start | bytes 448520 | tf_op jit(solution)/shard_map/ppermute | solution.py:314
  44.2 0.5 collective-permute-start.3
  44.7 2.1 %collective-permute-done.1.first = bf16[584,128]{1,0:T(8,128)(2,1)S(1)} collective-permute-done((bf16[584,128]{1,0:T(8,128)(2,1)S(1)}, bf16[584,128]{1,0:T(8,128)(2,1)S(1)}, u32[]{:S(2)}, u32[]{:S(2)}) %collective-permute-start.1) | collective-permute-done | bytes 149536 | tf_op jit(solution)/shard_map/ppermute | solution.py:314
  46.7 4.7 %collective-permute-done.2.second = bf16[584,128]{1,0:T(8,128)(2,1)S(1)} collective-permute-done((bf16[584,128]{1,0:T(8,128)(2,1)S(1)}, bf16[584,128]{1,0:T(8,128)(2,1)S(1)}, u32[]{:S(2)}, u32[]{:S(2)}) %collective-permute-start.2) | collective-permute-done | bytes 149536 | tf_op jit(solution)/shard_map/ppermute | solution.py:314
  51.4 2.4 %collective-permute-done.3.third = bf16[584,128]{1,0:T(8,128)(2,1)S(1)} collective-permute-done((bf16[584,128]{1,0:T(8,128)(2,1)S(1)}, bf16[584,128]{1,0:T(8,128)(2,1)S(1)}, u32[]{:S(2)}, u32[]{:S(2)}) %collective-permute-start.3) | collective-permute-done | bytes 149536 | tf_op jit(solution)/shard_map/ppermute | solution.py:314
  53.9 16.1 %all_to_all.20.slots = bf16[32,24,128]{2,1,0:T(8,128)(2,1)S(1)} all-to-all(bf16[32,24,128]{2,1,0:T(8,128)(2,1)S(1)} %bitcast.8), channel_id=1, replica_groups={{0,64,128,192,8,72,136,200,16,80,144,208,24,88,152,216,32,96,160,224,40..., dimensions={0} | all-to-all | bytes 393216 | tf_op jit(solution)/shard_map/all_to_all | solution.py:330
  70.1 14.5 %all_to_all.21 = bf16[32,24,128]{2,1,0:T(8,128)(2,1)S(1)} all-to-all(bf16[32,24,128]{2,1,0:T(8,128)(2,1)S(1)} %shard_map.114), channel_id=1, replica_groups={{0,64,128,192,8,72,136,200,16,80,144,208,24,88,152,216,32,96,160,224,40..., dimensions={0} | all-to-all | bytes 393216 | tf_op jit(solution)/shard_map/all_to_all | solution.py:330
  84.6 3.8 %all-to-all-start.1 = ((bf16[16,32,384]{2,1,0:T(8,128)(2,1)}), bf16[16,32,384]{2,1,0:T(8,128)(2,1)S(1)}, u32[]{:S(2)}, u32[]{:S(2)}) async-start(bf16[16,32,384]{2,1,0:T(8,128)(2,1)} %get-tuple-element.19), calls=%async_computation.1 | async-start | bytes 786432 | tf_op jit(solution)/shard_map/all_to_all | solution.py:327
  88.4 0.6 collective-permute-start.6
  88.9 0.5 collective-permute-start.5
  89.4 3.2 %collective-permute-start.4 = (bf16[584,128]{1,0:T(8,128)(2,1)S(1)}, bf16[584,128]{1,0:T(8,128)(2,1)S(1)}, u32[]{:S(2)}, u32[]{:S(2)}) collective-permute-start(bf16[584,128]{1,0:T(8,128)(2,1)S(1)} %slice.4.refs_3_), channel_id=1, source_target_pairs={{0,2},{1,3},{2,0},{3,1},{4,6},{5,7},{6,4},{7,5},{8,10},{9,11},{10,... | collective-permute-start | bytes 448520 | tf_op jit(solution)/shard_map/ppermute | solution.py:314
  92.5 3.9 %collective-permute-done.6.refs_6_ = bf16[584,128]{1,0:T(8,128)(2,1)S(1)} collective-permute-done((bf16[584,128]{1,0:T(8,128)(2,1)S(1)}, bf16[584,128]{1,0:T(8,128)(2,1)S(1)}, u32[]{:S(2)}, u32[]{:S(2)}) %collective-permute-start.6) | collective-permute-done | bytes 149536 | tf_op jit(solution)/shard_map/ppermute | solution.py:314
  96.4 0.5 collective-permute-start.9
  96.9 0.3 collective-permute-done.4.refs_4_
  97.3 3.2 %all-to-all-done.1.packed = bf16[16,32,384]{2,1,0:T(8,128)(2,1)S(1)} async-done(((bf16[16,32,384]{2,1,0:T(8,128)(2,1)}), bf16[16,32,384]{2,1,0:T(8,128)(2,1)S(1)}, u32[]{:S(2)}, u32[]{:S(2)}) %all-to-all-start.1) | async-done | bytes 393248 | tf_op jit(solution)/shard_map/all_to_all | solution.py:327
  100.5 0.9 shard_map.111
  101.4 1.6 %shard_map.115 = (f32[384,768]{1,0:T(8,128)}, f32[768,384]{1,0:T(8,128)}, f32[384]{0:T(512)}, f32[384]{0:T(512)}) custom-call(s32[1]{0:T(128)} %bitcast.core.refs_0_, s32[1]{0:T(128)} %bitcast.5.place.refs_1_, f32[1,384]{1,0:T(1,128)S(1)} %reshape.32.gate.refs_2_, bf16[584,128]{1,0:T(8,128)(2,1)S(1)} %slice.4.refs_3_, ...), custom_call_target="tpu_custom_call" | custom-call | tf_op jit(solution)/shard_map/pallas_call | solution.py:289
  (22 shorter events, 0.2 us)
Async XLA Ops:
  0.6 12.4 %copy-start.2 = (f32[384]{0:T(512)S(1)}, f32[384]{0:T(512)}, u32[]{:S(2)}) copy-start(f32[384]{0:T(512)} %param.11) | copy-start | bytes 4612
  0.6 12.4 %copy-start.3 = (f32[384]{0:T(512)S(1)}, f32[384]{0:T(512)}, u32[]{:S(2)}) copy-start(f32[384]{0:T(512)} %param.10) | copy-start | bytes 4612
  0.7 27.1 %copy-start.1 = (bf16[768,384]{1,0:T(8,128)(2,1)S(1)}, bf16[768,384]{1,0:T(8,128)(2,1)}, u32[]{:S(2)}) copy-start(bf16[768,384]{1,0:T(8,128)(2,1)} %merge.1) | copy-start | bytes 1769476
  0.7 27.1 %copy-start = (bf16[384,768]{1,0:T(8,128)(2,1)S(1)}, bf16[384,768]{1,0:T(8,128)(2,1)}, u32[]{:S(2)}) copy-start(bf16[384,768]{1,0:T(8,128)(2,1)} %spread.1) | copy-start | bytes 1769476
  2.7 25.0 %all-to-all-start = ((bf16[16,32,384]{2,1,0:T(8,128)(2,1)}), bf16[16,32,384]{2,1,0:T(8,128)(2,1)S(1)}, u32[]{:S(2)}, u32[]{:S(2)}) async-start(bf16[16,32,384]{2,1,0:T(8,128)(2,1)} %shard_map.109), calls=%async_computation | async-start | bytes 786432 | tf_op jit(solution)/shard_map/all_to_all | solution.py:327
  37.7 2.0 %collective-permute-start = (bf16[4,584,128]{2,1,0:T(8,128)(2,1)S(1)}, bf16[4,584,128]{2,1,0:T(8,128)(2,1)S(1)}, u32[]{:S(2)}, u32[]{:S(2)}) collective-permute-start(bf16[4,584,128]{2,1,0:T(8,128)(2,1)S(1)} %get-tuple-element.23), channel_id=1, source_target_pairs={{0,1},{1,0},{2,3},{3,2},{4,5},{5,4},{6,7},{7,6},{8,9},{9,8},{10,11... | collective-permute-start | bytes 1794056 | tf_op jit(solution)/shard_map/ppermute | solution.py:314
  39.9 6.8 %collective-permute-start.1 = (bf16[584,128]{1,0:T(8,128)(2,1)S(1)}, bf16[584,128]{1,0:T(8,128)(2,1)S(1)}, u32[]{:S(2)}, u32[]{:S(2)}) collective-permute-start(bf16[584,128]{1,0:T(8,128)(2,1)S(1)} %get-tuple-element.25), channel_id=1, source_target_pairs={{0,2},{1,3},{2,0},{3,1},{4,6},{5,7},{6,4},{7,5},{8,10},{9,11},{10,... | collective-permute-start | bytes 448520 | tf_op jit(solution)/shard_map/ppermute | solution.py:314
  41.4 10.0 %collective-permute-start.2 = (bf16[584,128]{1,0:T(8,128)(2,1)S(1)}, bf16[584,128]{1,0:T(8,128)(2,1)S(1)}, u32[]{:S(2)}, u32[]{:S(2)}) collective-permute-start(bf16[584,128]{1,0:T(8,128)(2,1)S(1)} %get-tuple-element.26), channel_id=1, source_target_pairs={{0,4},{1,5},{2,6},{3,7},{4,0},{5,1},{6,2},{7,3},{8,12},{9,13},{10,... | collective-permute-start | bytes 448520 | tf_op jit(solution)/shard_map/ppermute | solution.py:314
  44.2 9.6 %collective-permute-start.3 = (bf16[584,128]{1,0:T(8,128)(2,1)S(1)}, bf16[584,128]{1,0:T(8,128)(2,1)S(1)}, u32[]{:S(2)}, u32[]{:S(2)}) collective-permute-start(bf16[584,128]{1,0:T(8,128)(2,1)S(1)} %get-tuple-element.27), channel_id=1, source_target_pairs={{0,6},{1,7},{2,4},{3,5},{4,2},{5,3},{6,0},{7,1},{8,14},{9,15},{10,... | collective-permute-start | bytes 448520 | tf_op jit(solution)/shard_map/ppermute | solution.py:314
  84.6 15.9 %all-to-all-start.1 = ((bf16[16,32,384]{2,1,0:T(8,128)(2,1)}), bf16[16,32,384]{2,1,0:T(8,128)(2,1)S(1)}, u32[]{:S(2)}, u32[]{:S(2)}) async-start(bf16[16,32,384]{2,1,0:T(8,128)(2,1)} %get-tuple-element.19), calls=%async_computation.1 | async-start | bytes 786432 | tf_op jit(solution)/shard_map/all_to_all | solution.py:327
  88.4 8.1 %collective-permute-start.6 = (bf16[584,128]{1,0:T(8,128)(2,1)S(1)}, bf16[584,128]{1,0:T(8,128)(2,1)S(1)}, u32[]{:S(2)}, u32[]{:S(2)}) collective-permute-start(bf16[584,128]{1,0:T(8,128)(2,1)S(1)} %slice.4.refs_3_), channel_id=1, source_target_pairs={{0,6},{1,7},{2,4},{3,5},{4,2},{5,3},{6,0},{7,1},{8,14},{9,15},{10,... | collective-permute-start | bytes 448520 | tf_op jit(solution)/shard_map/ppermute | solution.py:314
  88.9 7.5 %collective-permute-start.5 = (bf16[584,128]{1,0:T(8,128)(2,1)S(1)}, bf16[584,128]{1,0:T(8,128)(2,1)S(1)}, u32[]{:S(2)}, u32[]{:S(2)}) collective-permute-start(bf16[584,128]{1,0:T(8,128)(2,1)S(1)} %slice.4.refs_3_), channel_id=1, source_target_pairs={{0,4},{1,5},{2,6},{3,7},{4,0},{5,1},{6,2},{7,3},{8,12},{9,13},{10,... | collective-permute-start | bytes 448520 | tf_op jit(solution)/shard_map/ppermute | solution.py:314
  89.4 7.9 %collective-permute-start.4 = (bf16[584,128]{1,0:T(8,128)(2,1)S(1)}, bf16[584,128]{1,0:T(8,128)(2,1)S(1)}, u32[]{:S(2)}, u32[]{:S(2)}) collective-permute-start(bf16[584,128]{1,0:T(8,128)(2,1)S(1)} %slice.4.refs_3_), channel_id=1, source_target_pairs={{0,2},{1,3},{2,0},{3,1},{4,6},{5,7},{6,4},{7,5},{8,10},{9,11},{10,... | collective-permute-start | bytes 448520 | tf_op jit(solution)/shard_map/ppermute | solution.py:314
  92.5 8.9 %collective-permute-start.7 = (bf16[584,128]{1,0:T(8,128)(2,1)S(1)}, bf16[584,128]{1,0:T(8,128)(2,1)S(1)}, u32[]{:S(2)}, u32[]{:S(2)}) collective-permute-start(bf16[584,128]{1,0:T(8,128)(2,1)S(1)} %slice.4.refs_3_), channel_id=1, source_target_pairs={{0,1},{1,0},{2,3},{3,2},{4,5},{5,4},{6,7},{7,6},{8,9},{9,8},{10,11... | collective-permute-start | bytes 448520 | tf_op jit(solution)/shard_map/ppermute | solution.py:314
  96.4 5.0 %collective-permute-start.10 = (bf16[584,128]{1,0:T(8,128)(2,1)S(1)}, bf16[584,128]{1,0:T(8,128)(2,1)S(1)}, u32[]{:S(2)}, u32[]{:S(2)}) collective-permute-start(bf16[584,128]{1,0:T(8,128)(2,1)S(1)} %collective-permute-done.6.refs_6_), channel_id=1, source_target_pairs={{0,1},{1,0},{2,3},{3,2},{4,5},{5,4},{6,7},{7,6},{8,9},{9,8},{10,11... | collective-permute-start | bytes 448520 | tf_op jit(solution)/shard_map/ppermute | solution.py:314
  96.4 5.0 %collective-permute-start.9 = (bf16[584,128]{1,0:T(8,128)(2,1)S(1)}, bf16[584,128]{1,0:T(8,128)(2,1)S(1)}, u32[]{:S(2)}, u32[]{:S(2)}) collective-permute-start(bf16[584,128]{1,0:T(8,128)(2,1)S(1)} %collective-permute-done.5.refs_5_), channel_id=1, source_target_pairs={{0,1},{1,0},{2,3},{3,2},{4,5},{5,4},{6,7},{7,6},{8,9},{9,8},{10,11... | collective-permute-start | bytes 448520 | tf_op jit(solution)/shard_map/ppermute | solution.py:314
  97.3 4.1 %collective-permute-start.8 = (bf16[584,128]{1,0:T(8,128)(2,1)S(1)}, bf16[584,128]{1,0:T(8,128)(2,1)S(1)}, u32[]{:S(2)}, u32[]{:S(2)}) collective-permute-start(bf16[584,128]{1,0:T(8,128)(2,1)S(1)} %collective-permute-done.4.refs_4_), channel_id=1, source_target_pairs={{0,1},{1,0},{2,3},{3,2},{4,5},{5,4},{6,7},{7,6},{8,9},{9,8},{10,11... | collective-permute-start | bytes 448520 | tf_op jit(solution)/shard_map/ppermute | solution.py:314

commit v3 on v2

v3 whole, which is shorter than its diff:
```python
import math

import jax
import jax.numpy as jnp
from jax import lax
from jax.experimental import pallas as pl
from jax.experimental.pallas import tpu as pltpu
from jax.sharding import PartitionSpec as P


SECTIONS = 4
MEMBERS = 16
ROWS = 32
UNITS = 192
SWITCH = 384
HIDDEN = 768
PAIRS = 256
PIECE = 144
AUX = 8
BLOCK = 32
ORDER = list(reversed(range(MEMBERS)))

sqrt_half = 0.7071067811865476
inv_sqrt_two_pi = 0.3989422804014327
f32 = jnp.float32
bf16 = jnp.bfloat16


def dot(a, b, ca, cb):
    return lax.dot_general(a, b, (((ca,), (cb,)), ((), ())), preferred_element_type=f32)


def sides(section):
    bit = MEMBERS >> (section + 1)
    lower = [g for g in range(MEMBERS) if not g & bit]
    return lower, [g + bit for g in lower]


def load_rows(ref, members):
    return jnp.concatenate([ref[g] for g in members], 0)


def store_rows(ref, members, value):
    for k, g in enumerate(members):
        ref[g] = value[ROWS * k : ROWS * (k + 1)]


def add_to(ref, section, term):
    if section == SECTIONS - 1:
        ref[...] = term
    else:
        ref[...] += term


def switch_kernel(
    core,
    packed,
    spread,
    merge,
    bias,
    gate,
    packed_out,
    send,
    keep,
    state,
    grad,
    paired,
    pre,
    normed,
    slope,
    hidden,
    scale,
    dbranch,
    dpre,
    spread_sum,
    merge_sum,
):
    gate_open = jax.nn.sigmoid(gate[...].reshape(1, SWITCH))
    bias_all = 0.25 * bias[...].reshape(1, SWITCH)
    for i, g in enumerate(ORDER):
        state[g] = packed[i, :, :UNITS]
        grad[g] = packed[i, :, UNITS:]
    for section in range(SECTIONS):
        lower, upper = sides(section)
        base = PAIRS * section
        rows = slice(base, base + PAIRS)
        paired[rows, :UNITS] = load_rows(state, lower)
        paired[rows, UNITS:] = load_rows(state, upper)
        here = paired[rows, :]
        pre[...] = dot(here, spread[...], 1, 0)
        for start in range(0, PAIRS, BLOCK):
            at = slice(start, start + BLOCK)
            to = slice(base + start, base + start + BLOCK)
            value = pre[at, :]
            centered = value - jnp.mean(value, -1, keepdims=True)
            inv = lax.rsqrt(jnp.mean(centered * centered, -1, keepdims=True) + 1e-05)
            norm = centered * inv
            cdf = 0.5 * (1.0 + lax.erf(norm * sqrt_half))
            normed[to, :] = norm
            slope[to, :] = cdf + norm * jnp.exp(-0.5 * norm * norm) * inv_sqrt_two_pi
            hidden[to, :] = (norm * cdf).astype(bf16)
            scale[to, :] = jnp.broadcast_to(inv, (BLOCK, 128))
        branch = dot(hidden[rows, :], merge[...], 1, 0)
        out = (gate_open * here.astype(f32) + (0.25 * branch + bias_all)).astype(bf16)
        store_rows(state, lower, out[:, :UNITS])
        store_rows(state, upper, out[:, UNITS:])
    for i, g in enumerate(ORDER):
        packed_out[i, :, :UNITS] = state[g]

    bias_sum = jnp.zeros((1, SWITCH), f32)
    gate_sum = jnp.zeros((1, SWITCH), f32)
    for section in reversed(range(SECTIONS)):
        lower, upper = sides(section)
        base = PAIRS * section
        rows = slice(base, base + PAIRS)
        dbranch[rows, :UNITS] = load_rows(grad, lower)
        dbranch[rows, UNITS:] = load_rows(grad, upper)
        wide = dbranch[rows, :].astype(f32)
        bias_sum += jnp.sum(wide, 0, keepdims=True)
        gate_sum += jnp.sum(wide * paired[rows, :].astype(f32), 0, keepdims=True)
        quarter = (0.25 * wide).astype(bf16)
        dbranch[rows, :] = quarter
        pre[...] = dot(quarter, merge[...], 1, 1)
        add_to(merge_sum, section, dot(hidden[rows, :], quarter, 0, 0))
        for start in range(0, PAIRS, BLOCK):
            at = slice(start, start + BLOCK)
            to = slice(base + start, base + start + BLOCK)
            norm = normed[to, :]
            dn = pre[at, :] * slope[to, :]
            mean = jnp.mean(dn, -1, keepdims=True)
            along = jnp.mean(dn * norm, -1, keepdims=True)
            inv = scale[to, :][:, :1]
            dpre[at, :] = (inv * (dn - mean - norm * along)).astype(bf16)
        back = dpre[...]
        total = (gate_open * wide + dot(back, spread[...], 1, 1)).astype(bf16)
        store_rows(grad, lower, total[:, :UNITS])
        store_rows(grad, upper, total[:, UNITS:])
        add_to(spread_sum, section, dot(paired[rows, :], back, 0, 0))
    for i, g in enumerate(ORDER):
        packed_out[i, :, UNITS:] = grad[g]

    bias_row = 0.25 * bias_sum
    gate_row = gate_sum
    aux = jnp.concatenate(
        [row[:, 128 * k : 128 * (k + 1)] for row in (bias_row, gate_row) for k in range(3)]
        + [jnp.zeros((2, 128), f32)],
        0,
    )

    def put_spread(ref):
        for p in range(16):
            for c in range(6):
                ref[p, 24 * c : 24 * (c + 1), :] = spread_sum[
                    24 * p : 24 * (p + 1), 128 * c : 128 * (c + 1)
                ].astype(ref.dtype)
        ref[0, PIECE:, :] = aux.astype(ref.dtype)
        ref[1:, PIECE:, :] = jnp.zeros((15, AUX, 128), ref.dtype)

    def put_merge(ref):
        for p in range(16):
            for c in range(3):
                ref[p, 48 * c : 48 * (c + 1), :] = merge_sum[
                    48 * p : 48 * (p + 1), 128 * c : 128 * (c + 1)
                ].astype(ref.dtype)
        ref[:, PIECE:, :] = jnp.zeros((16, AUX, 128), ref.dtype)

    @pl.when(core[0] == 0)
    def _():
        put_spread(keep)
        put_merge(send)

    @pl.when(core[0] != 0)
    def _():
        put_merge(keep)
        put_spread(send)


def pack_kernel(tokens, out_grad, packed):
    rows = jnp.concatenate([tokens[...], out_grad[...]], 0).T
    for i, g in enumerate(ORDER):
        packed[i] = rows[ROWS * g : ROWS * (g + 1)]


def unpack_kernel(packed, network_out, token_grad):
    places = [ORDER.index(g) for g in range(MEMBERS)]
    columns = jnp.concatenate([packed[i] for i in places], 0).T
    network_out[...] = columns[:UNITS]
    token_grad[...] = columns[UNITS:]


def core_sum_kernel(keep, came, pieces):
    pieces[...] = (keep[...] + came[...].astype(f32)).astype(bf16)


def piece_sum_kernel(pieces, total):
    value = pieces[0].astype(f32)
    for k in range(1, pieces.shape[0]):
        value = value + pieces[k].astype(f32)
    total[...] = value.astype(bf16)


def pair_sum_kernel(own, came, total):
    value = (own[...].astype(f32) + came[...].astype(f32)).astype(bf16)
    total[...] = jnp.broadcast_to(value, total.shape)


def finish_kernel(core, gate, mine, theirs, spread, merge, bias, gate_out, *, grad_scale):
    def write(first, second):
        for p in range(16):
            rows = slice(24 * p, 24 * (p + 1))
            for c in range(6):
                spread[rows, 128 * c : 128 * (c + 1)] = (
                    first[p, 24 * c : 24 * (c + 1), :].astype(f32) * grad_scale
                )
            rows = slice(48 * p, 48 * (p + 1))
            for c in range(3):
                merge[rows, 128 * c : 128 * (c + 1)] = (
                    second[p, 48 * c : 48 * (c + 1), :].astype(f32) * grad_scale
                )
        aux = first[0, PIECE:, :].astype(f32) * grad_scale
        gate_open = jax.nn.sigmoid(gate[...].reshape(1, SWITCH))
        slope = gate_open * (1.0 - gate_open)
        for k in range(3):
            at = slice(128 * k, 128 * (k + 1))
            bias[at] = aux[k, :]
            gate_out[at] = aux[3 + k, :] * slope[0, at]

    @pl.when(core[0] == 0)
    def _():
        write(mine, theirs)

    @pl.when(core[0] != 0)
    def _():
        write(theirs, mine)


def shaped(shape, dtype):
    return jax.ShapeDtypeStruct(shape, dtype)


def near(shape, dtype):
    return pltpu.VMEM(shape, dtype)


VMEM = pl.BlockSpec(memory_space=pltpu.VMEM)
SMEM = pl.BlockSpec(memory_space=pltpu.SMEM)


def call(kernel, outs, ins, scalars=0, scratch=(), far=False):
    arrays = ins[scalars:]
    space = pltpu.HBM if far else pltpu.VMEM
    arrays = [pltpu.with_memory_space_constraint(a, space) for a in arrays]
    return pl.pallas_call(
        kernel,
        out_shape=outs,
        in_specs=[SMEM] * scalars + [VMEM] * len(arrays),
        out_specs=tuple(VMEM for _ in outs) if isinstance(outs, tuple) else VMEM,
        scratch_shapes=list(scratch),
        compiler_params=pltpu.CompilerParams(vmem_limit_bytes=40 * 2**20),
    )(*ins[:scalars], *arrays)


def bit_groups(count, bits):
    mask = sum(1 << b for b in bits)
    groups = []
    for base in range(count):
        if base & mask:
            continue
        group = [base]
        for b in sorted(bits):
            group = group + [g | (1 << b) for g in group]
        groups.append(group)
    return groups


def exchange(value, mask):
    return lax.ppermute(value, "seq", [(i, i ^ mask) for i in range(lax.axis_size("seq"))])


def step(tokens, out_grad, spread_weight, merge_weight, switch_bias, gate_logit):
    count = lax.axis_size("seq")
    grad_scale = 1.0 / math.sqrt(count * tokens.shape[0])
    position = lax.axis_index("seq")
    core = (position % 2).astype(jnp.int32).reshape(1)
    members = [[group[g] for g in ORDER] for group in bit_groups(count, (4, 5, 6, 7))]
    planes = bit_groups(count, (1, 2, 6, 7))

    def swap_rows(packed):
        return lax.all_to_all(packed, "seq", 0, 0, axis_index_groups=members)

    def swap_slots(slots):
        return lax.all_to_all(slots, "seq", 0, 0, axis_index_groups=planes)

    rows = tokens.shape[0]
    packed = call(
        pack_kernel,
        near((MEMBERS, ROWS, SWITCH), bf16),
        (tokens.T, out_grad.T),
        far=True,
    )
    packed = swap_rows(packed)
    total = SECTIONS * PAIRS
    piece = (PIECE + AUX, 128)
    half = (16, *piece)
    packed_out, send, keep = call(
        switch_kernel,
        (near((MEMBERS, ROWS, SWITCH), bf16), near(half, bf16), near(half, f32)),
        (core, packed, spread_weight, merge_weight, switch_bias, gate_logit),
        1,
        [
            pltpu.VMEM((MEMBERS, ROWS, UNITS), bf16),
            pltpu.VMEM((MEMBERS, ROWS, UNITS), bf16),
            pltpu.VMEM((total, SWITCH), bf16),
            pltpu.VMEM((PAIRS, HIDDEN), f32),
            pltpu.VMEM((total, HIDDEN), f32),
            pltpu.VMEM((total, HIDDEN), f32),
            pltpu.VMEM((total, HIDDEN), bf16),
            pltpu.VMEM((total, 128), f32),
            pltpu.VMEM((total, SWITCH), bf16),
            pltpu.VMEM((PAIRS, HIDDEN), bf16),
            pltpu.VMEM((SWITCH, HIDDEN), f32),
            pltpu.VMEM((HIDDEN, SWITCH), f32),
        ],
    )
    came = exchange(send, 1)
    pieces = call(core_sum_kernel, near(half, bf16), (keep, came))
    pieces = swap_slots(pieces)
    summed = call(piece_sum_kernel, near(piece, bf16), (pieces,))
    came = exchange(summed, 8)
    packed_out = swap_rows(packed_out)
    summed = call(pair_sum_kernel, near(piece, bf16), (summed, came))
    came = exchange(summed, 16)
    summed = call(pair_sum_kernel, near(piece, bf16), (summed, came))
    came = exchange(summed, 32)
    pieces = call(pair_sum_kernel, near(half, bf16), (summed, came))
    mine = swap_slots(pieces)
    theirs = exchange(mine, 1)
    network_out, token_grad = call(
        unpack_kernel, (shaped((UNITS, rows), bf16),) * 2, (packed_out,)
    )
    spread_grad, merge_grad, bias_grad, gate_grad = call(
        lambda *refs: finish_kernel(*refs, grad_scale=grad_scale),
        (
            shaped((SWITCH, HIDDEN), f32),
            shaped((HIDDEN, SWITCH), f32),
            shaped((SWITCH,), f32),
            shaped((SWITCH,), f32),
        ),
        (core, gate_logit, mine, theirs),
        1,
    )
    return (network_out.T, token_grad.T, spread_grad, merge_grad, bias_grad, gate_grad)


def solution(mesh):
    placed = (P("seq", None), P("seq", None), P(), P(), P(), P())
    return jax.shard_map(
        step,
        mesh=mesh,
        in_specs=placed,
        out_specs=(P("seq", None), P("seq", None), P(), P(), P(), P()),
        check_vma=False,
    )
```

time: 104 us -> 107 us (1.029)
  starting transfers between devices: 23.5 us -> 27.5 us
  waiting for transfers between devices: 33.3 us -> 30.7 us
  blocking collectives: 30.6 us -> 31.9 us
    all_to_all x2, starting transfers between devices: 14.1 us -> 20.1 us  [swap_rows(): return lax.all_to_all(packed, 'seq', 0, 0, axis_index_groups=members)]
    ppermute x11 -> x5, waiting for transfers between devices: 15.4 us -> 11.7 us  [exchange(): lax.ppermute(value, 'seq', [(i, i ^ mask) for i in range(lax.axis_size('s...]
    ppermute x11 -> x5, starting transfers between devices: 9.48 us -> 7.39 us  [exchange(): lax.ppermute(value, 'seq', [(i, i ^ mask) for i in range(lax.axis_size('s...]
    all_to_all x2, blocking collectives: 30.6 us -> 31.9 us  [swap_slots(): return lax.all_to_all(slots, 'seq', 0, 0, axis_index_groups=planes)]
    all_to_all x2, waiting for transfers between devices: 17.9 us -> 19 us  [swap_rows(): return lax.all_to_all(packed, 'seq', 0, 0, axis_index_groups=members)]
    pallas_call x7 -> x9, Pallas kernels: 14.8 us -> 14.4 us  [call(): pl.pallas_call(kernel, out_shape=outs, in_specs=[SMEM] * scalars + [VMEM]...]
  transfers between devices with their start and end apart: 13 -> 7, of which waited for: 8 -> 6; matrix products, arithmetic and copies ran while one was open for 0% -> 0% of each run, Pallas kernels for 1% -> 1%
where the time goes in v3:
time: 107 us; the launch traced here: 105 us
  blocking collectives  31.9 us (30%)
  waiting for transfers between devices  30.7 us (29%)
  starting transfers between devices  27.5 us (26%)
  Pallas kernels  14.4 us (13%)
    all_to_all x2, blocking collectives, swap_slots(): return lax.all_to_all(slots, 'seq', 0, 0, axis_index_groups=planes)  31.9 us
    all_to_all x2, starting transfers between devices, swap_rows(): return lax.all_to_all(packed, 'seq', 0, 0, axis_index_groups=members)  20.1 us
    all_to_all x2, waiting for transfers between devices, swap_rows(): return lax.all_to_all(packed, 'seq', 0, 0, axis_index_groups=members)  19 us
    pallas_call x9, Pallas kernels, call(): pl.pallas_call(kernel, out_shape=outs, in_specs=[SMEM] * scalars + [VMEM]...  14.4 us
    ppermute x5, waiting for transfers between devices, exchange(): lax.ppermute(value, 'seq', [(i, i ^ mask) for i in range(lax.axis_size('s...  11.7 us
    ppermute x5, starting transfers between devices, exchange(): lax.ppermute(value, 'seq', [(i, i ^ mask) for i in range(lax.axis_size('s...  7.39 us
  transfers between devices with their start and end apart: 7, of which 6 were waited for; matrix products, arithmetic and copies ran while one was open for 0% of the time, Pallas kernels for 1%

profile of v3, /device:TPU:32, one launch (start us, length us, event | category | flops | bytes accessed | tf_op | source)
XLA Modules:
  0.0 105.2 jit_solution(15325910185027963054)
XLA Ops:
  0.6 0.0 copy-start.2
  0.7 2.0 %shard_map.109 = bf16[16,32,384]{2,1,0:T(8,128)(2,1)} custom-call(bf16[192,512]{1,0:T(8,128)(2,1)} %bitcast.5, bf16[192,512]{1,0:T(8,128)(2,1)} %bitcast.6), custom_call_target="tpu_custom_call" | custom-call | tf_op jit(solution)/shard_map/pallas_call | solution.py:253
  2.7 11.3 %all-to-all-start = ((bf16[16,32,384]{2,1,0:T(8,128)(2,1)}), bf16[16,32,384]{2,1,0:T(8,128)(2,1)S(1)}, u32[]{:S(2)}, u32[]{:S(2)}) async-start(bf16[16,32,384]{2,1,0:T(8,128)(2,1)} %shard_map.109), calls=%async_computation | async-start | bytes 786432 | tf_op jit(solution)/shard_map/all_to_all | solution.py:289
  14.0 10.9 %all-to-all-done.packed = bf16[16,32,384]{2,1,0:T(8,128)(2,1)S(1)} async-done(((bf16[16,32,384]{2,1,0:T(8,128)(2,1)}), bf16[16,32,384]{2,1,0:T(8,128)(2,1)S(1)}, u32[]{:S(2)}, u32[]{:S(2)}) %all-to-all-start) | async-done | bytes 393248 | tf_op jit(solution)/shard_map/all_to_all | solution.py:289
  24.9 0.0 copy-done.3
  24.9 9.5 %shard_map.110 = (bf16[16,32,384]{2,1,0:T(8,128)(2,1)}, bf16[16,152,128]{2,1,0:T(8,128)(2,1)S(1)}, f32[16,152,128]{2,1,0:T(8,128)S(1)}) custom-call(s32[1]{0:T(128)} %bitcast.core.refs_0_, bf16[16,32,384]{2,1,0:T(8,128)(2,1)S(1)} %all-to-all-done.packed, bf16[384,768]{1,0:T(8,128)(2,1)S(1)} %copy-done, bf16[768,384]{1,0:T(8,128)(2,1)S(1)} %copy-done.1, ...), custom_call_target="tpu_custom_call" | custom-call | tf_op jit(solution)/shard_map/pallas_call | solution.py:253
  34.5 0.0 collective-permute-start
  34.5 2.0 %collective-permute-done.came = bf16[16,152,128]{2,1,0:T(8,128)(2,1)S(1)} collective-permute-done((bf16[16,152,128]{2,1,0:T(8,128)(2,1)S(1)}, bf16[16,152,128]{2,1,0:T(8,128)(2,1)S(1)}, u32[]{:S(2)}, u32[]{:S(2)}) %collective-permute-start) | collective-permute-done | bytes 622624 | tf_op jit(solution)/shard_map/ppermute | solution.py:277
  36.5 0.2 shard_map.112
  36.7 18.1 %all_to_all.20.pieces = bf16[16,152,128]{2,1,0:T(8,128)(2,1)S(1)} all-to-all(bf16[16,152,128]{2,1,0:T(8,128)(2,1)S(1)} %shard_map.112), channel_id=1, replica_groups={{0,2,4,6,64,66,68,70,128,130,132,134,192,194,196,198},{1,3,5,7,65,67,69..., dimensions={0} | all-to-all | bytes 1245184 | tf_op jit(solution)/shard_map/all_to_all | solution.py:292
  54.8 0.1 shard_map.113.own
  54.9 1.9 %collective-permute-start.1 = (bf16[152,128]{1,0:T(8,128)(2,1)S(1)}, bf16[152,128]{1,0:T(8,128)(2,1)S(1)}, u32[]{:S(2)}, u32[]{:S(2)}) collective-permute-start(bf16[152,128]{1,0:T(8,128)(2,1)S(1)} %shard_map.113.own), channel_id=1, source_target_pairs={{0,8},{1,9},{2,10},{3,11},{4,12},{5,13},{6,14},{7,15},{8,0},{9,1},... | collective-permute-start | bytes 116744 | tf_op jit(solution)/shard_map/ppermute | solution.py:277
  56.8 2.2 %collective-permute-done.1.came = bf16[152,128]{1,0:T(8,128)(2,1)S(1)} collective-permute-done((bf16[152,128]{1,0:T(8,128)(2,1)S(1)}, bf16[152,128]{1,0:T(8,128)(2,1)S(1)}, u32[]{:S(2)}, u32[]{:S(2)}) %collective-permute-start.1) | collective-permute-done | bytes 38944 | tf_op jit(solution)/shard_map/ppermute | solution.py:277
  59.0 1.1 %collective-permute-start.2 = (bf16[152,128]{1,0:T(8,128)(2,1)S(1)}, bf16[152,128]{1,0:T(8,128)(2,1)S(1)}, u32[]{:S(2)}, u32[]{:S(2)}) collective-permute-start(bf16[152,128]{1,0:T(8,128)(2,1)S(1)} %shard_map.114.own), channel_id=1, source_target_pairs={{0,16},{1,17},{2,18},{3,19},{4,20},{5,21},{6,22},{7,23},{8,24},{9,... | collective-permute-start | bytes 116744 | tf_op jit(solution)/shard_map/ppermute | solution.py:277
  60.1 3.8 %collective-permute-done.2.came = bf16[152,128]{1,0:T(8,128)(2,1)S(1)} collective-permute-done((bf16[152,128]{1,0:T(8,128)(2,1)S(1)}, bf16[152,128]{1,0:T(8,128)(2,1)S(1)}, u32[]{:S(2)}, u32[]{:S(2)}) %collective-permute-start.2) | collective-permute-done | bytes 38944 | tf_op jit(solution)/shard_map/ppermute | solution.py:277
  64.0 4.3 %collective-permute-start.3 = (bf16[152,128]{1,0:T(8,128)(2,1)S(1)}, bf16[152,128]{1,0:T(8,128)(2,1)S(1)}, u32[]{:S(2)}, u32[]{:S(2)}) collective-permute-start(bf16[152,128]{1,0:T(8,128)(2,1)S(1)} %shard_map.115.own), channel_id=1, source_target_pairs={{0,32},{1,33},{2,34},{3,35},{4,36},{5,37},{6,38},{7,39},{8,40},{9,... | collective-permute-start | bytes 116744 | tf_op jit(solution)/shard_map/ppermute | solution.py:277
  68.3 3.6 %collective-permute-done.3.came = bf16[152,128]{1,0:T(8,128)(2,1)S(1)} collective-permute-done((bf16[152,128]{1,0:T(8,128)(2,1)S(1)}, bf16[152,128]{1,0:T(8,128)(2,1)S(1)}, u32[]{:S(2)}, u32[]{:S(2)}) %collective-permute-start.3) | collective-permute-done | bytes 38944 | tf_op jit(solution)/shard_map/ppermute | solution.py:277
  72.0 13.8 %all_to_all.21.refs_2_ = bf16[16,152,128]{2,1,0:T(8,128)(2,1)S(1)} all-to-all(bf16[16,152,128]{2,1,0:T(8,128)(2,1)S(1)} %shard_map.116), channel_id=1, replica_groups={{0,2,4,6,64,66,68,70,128,130,132,134,192,194,196,198},{1,3,5,7,65,67,69..., dimensions={0} | all-to-all | bytes 1245184 | tf_op jit(solution)/shard_map/all_to_all | solution.py:292
  85.8 8.8 %all-to-all-start.1 = ((bf16[16,32,384]{2,1,0:T(8,128)(2,1)}), bf16[16,32,384]{2,1,0:T(8,128)(2,1)S(1)}, u32[]{:S(2)}, u32[]{:S(2)}) async-start(bf16[16,32,384]{2,1,0:T(8,128)(2,1)} %get-tuple-element.15), calls=%async_computation.1 | async-start | bytes 786432 | tf_op jit(solution)/shard_map/all_to_all | solution.py:289
  94.6 0.0 collective-permute-start.4
  94.6 8.1 %all-to-all-done.1.packed = bf16[16,32,384]{2,1,0:T(8,128)(2,1)S(1)} async-done(((bf16[16,32,384]{2,1,0:T(8,128)(2,1)}), bf16[16,32,384]{2,1,0:T(8,128)(2,1)S(1)}, u32[]{:S(2)}, u32[]{:S(2)}) %all-to-all-start.1) | async-done | bytes 393248 | tf_op jit(solution)/shard_map/all_to_all | solution.py:289
  102.7 0.9 shard_map.111
  103.5 0.0 collective-permute-done.4.refs_3_
  103.6 1.6 %shard_map.117 = (f32[384,768]{1,0:T(8,128)}, f32[768,384]{1,0:T(8,128)}, f32[384]{0:T(512)}, f32[384]{0:T(512)}) custom-call(s32[1]{0:T(128)} %bitcast.core.refs_0_, f32[384]{0:T(512)S(1)} %copy-done.2, bf16[16,152,128]{2,1,0:T(8,128)(2,1)S(1)} %all_to_all.21.refs_2_, bf16[16,152,128]{2,1,0:T(8,128)(2,1)S(1)} %collective-permute-done.4.refs_3_), custom_call_target="tpu_custom_call" | custom-call | tf_op jit(solution)/shard_map/pallas_call | solution.py:253
  (9 shorter events, 0.1 us)
Async XLA Ops:
  0.6 24.3 %copy-start.2 = (f32[384]{0:T(512)S(1)}, f32[384]{0:T(512)}, u32[]{:S(2)}) copy-start(f32[384]{0:T(512)} %refs_1_.1) | copy-start | bytes 4612
  0.6 24.3 %copy-start.3 = (f32[384]{0:T(512)S(1)}, f32[384]{0:T(512)}, u32[]{:S(2)}) copy-start(f32[384]{0:T(512)} %bias.1) | copy-start | bytes 4612
  0.7 24.3 %copy-start.1 = (bf16[768,384]{1,0:T(8,128)(2,1)S(1)}, bf16[768,384]{1,0:T(8,128)(2,1)}, u32[]{:S(2)}) copy-start(bf16[768,384]{1,0:T(8,128)(2,1)} %merge.1) | copy-start | bytes 1769476
  0.7 24.3 %copy-start = (bf16[384,768]{1,0:T(8,128)(2,1)S(1)}, bf16[384,768]{1,0:T(8,128)(2,1)}, u32[]{:S(2)}) copy-start(bf16[384,768]{1,0:T(8,128)(2,1)} %spread.1) | copy-start | bytes 1769476
  2.7 22.2 %all-to-all-start = ((bf16[16,32,384]{2,1,0:T(8,128)(2,1)}), bf16[16,32,384]{2,1,0:T(8,128)(2,1)S(1)}, u32[]{:S(2)}, u32[]{:S(2)}) async-start(bf16[16,32,384]{2,1,0:T(8,128)(2,1)} %shard_map.109), calls=%async_computation | async-start | bytes 786432 | tf_op jit(solution)/shard_map/all_to_all | solution.py:289
  34.5 2.1 %collective-permute-start = (bf16[16,152,128]{2,1,0:T(8,128)(2,1)S(1)}, bf16[16,152,128]{2,1,0:T(8,128)(2,1)S(1)}, u32[]{:S(2)}, u32[]{:S(2)}) collective-permute-start(bf16[16,152,128]{2,1,0:T(8,128)(2,1)S(1)} %get-tuple-element.19), channel_id=1, source_target_pairs={{0,1},{1,0},{2,3},{3,2},{4,5},{5,4},{6,7},{7,6},{8,9},{9,8},{10,11... | collective-permute-start | bytes 1867784 | tf_op jit(solution)/shard_map/ppermute | solution.py:277
  54.9 4.1 %collective-permute-start.1 = (bf16[152,128]{1,0:T(8,128)(2,1)S(1)}, bf16[152,128]{1,0:T(8,128)(2,1)S(1)}, u32[]{:S(2)}, u32[]{:S(2)}) collective-permute-start(bf16[152,128]{1,0:T(8,128)(2,1)S(1)} %shard_map.113.own), channel_id=1, source_target_pairs={{0,8},{1,9},{2,10},{3,11},{4,12},{5,13},{6,14},{7,15},{8,0},{9,1},... | collective-permute-start | bytes 116744 | tf_op jit(solution)/shard_map/ppermute | solution.py:277
  59.0 5.0 %collective-permute-start.2 = (bf16[152,128]{1,0:T(8,128)(2,1)S(1)}, bf16[152,128]{1,0:T(8,128)(2,1)S(1)}, u32[]{:S(2)}, u32[]{:S(2)}) collective-permute-start(bf16[152,128]{1,0:T(8,128)(2,1)S(1)} %shard_map.114.own), channel_id=1, source_target_pairs={{0,16},{1,17},{2,18},{3,19},{4,20},{5,21},{6,22},{7,23},{8,24},{9,... | collective-permute-start | bytes 116744 | tf_op jit(solution)/shard_map/ppermute | solution.py:277
  64.0 8.0 %collective-permute-start.3 = (bf16[152,128]{1,0:T(8,128)(2,1)S(1)}, bf16[152,128]{1,0:T(8,128)(2,1)S(1)}, u32[]{:S(2)}, u32[]{:S(2)}) collective-permute-start(bf16[152,128]{1,0:T(8,128)(2,1)S(1)} %shard_map.115.own), channel_id=1, source_target_pairs={{0,32},{1,33},{2,34},{3,35},{4,36},{5,37},{6,38},{7,39},{8,40},{9,... | collective-permute-start | bytes 116744 | tf_op jit(solution)/shard_map/ppermute | solution.py:277
  85.8 16.9 %all-to-all-start.1 = ((bf16[16,32,384]{2,1,0:T(8,128)(2,1)}), bf16[16,32,384]{2,1,0:T(8,128)(2,1)S(1)}, u32[]{:S(2)}, u32[]{:S(2)}) async-start(bf16[16,32,384]{2,1,0:T(8,128)(2,1)} %get-tuple-element.15), calls=%async_computation.1 | async-start | bytes 786432 | tf_op jit(solution)/shard_map/all_to_all | solution.py:289
  94.6 9.0 %collective-permute-start.4 = (bf16[16,152,128]{2,1,0:T(8,128)(2,1)S(1)}, bf16[16,152,128]{2,1,0:T(8,128)(2,1)S(1)}, u32[]{:S(2)}, u32[]{:S(2)}) collective-permute-start(bf16[16,152,128]{2,1,0:T(8,128)(2,1)S(1)} %all_to_all.21.refs_2_), channel_id=1, source_target_pairs={{0,1},{1,0},{2,3},{3,2},{4,5},{5,4},{6,7},{7,6},{8,9},{9,8},{10,11... | collective-permute-start | bytes 1867784 | tf_op jit(solution)/shard_map/ppermute | solution.py:277

commit v4 on v3

--- a/solution.py
+++ b/solution.py
@@ -283,7 +283,10 @@
     position = lax.axis_index("seq")
     core = (position % 2).astype(jnp.int32).reshape(1)
     members = [[group[g] for g in ORDER] for group in bit_groups(count, (4, 5, 6, 7))]
-    planes = bit_groups(count, (1, 2, 6, 7))
+    planes = [
+        [group[15 - (4 * i % 16 + i // 4)] for i in range(16)]
+        for group in bit_groups(count, (1, 2, 6, 7))
+    ]
 
     def swap_rows(packed):
         return lax.all_to_all(packed, "seq", 0, 0, axis_index_groups=members)

time: 107 us -> 105 us (0.981)
  blocking collectives: 31.9 us -> 30.8 us
    ppermute x5, waiting for transfers between devices: 11.7 us -> 12.8 us  [exchange(): lax.ppermute(value, 'seq', [(i, i ^ mask) for i in range(lax.axis_size('s...]
    all_to_all x2, blocking collectives: 31.9 us -> 30.8 us  [swap_slots(): return lax.all_to_all(slots, 'seq', 0, 0, axis_index_groups=planes)]
    ppermute x5, starting transfers between devices: 7.39 us -> 6.3 us  [exchange(): lax.ppermute(value, 'seq', [(i, i ^ mask) for i in range(lax.axis_size('s...]
where the time goes in v4:
time: 105 us; the launch traced here: 104 us
  waiting for transfers between devices  31.7 us (30%)
  blocking collectives  30.8 us (29%)
  starting transfers between devices  26.5 us (25%)
  Pallas kernels  14.4 us (14%)
    all_to_all x2, blocking collectives, swap_slots(): return lax.all_to_all(slots, 'seq', 0, 0, axis_index_groups=planes)  30.8 us
    all_to_all x2, starting transfers between devices, swap_rows(): return lax.all_to_all(packed, 'seq', 0, 0, axis_index_groups=members)  20.2 us
    all_to_all x2, waiting for transfers between devices, swap_rows(): return lax.all_to_all(packed, 'seq', 0, 0, axis_index_groups=members)  18.9 us
    pallas_call x9, Pallas kernels, call(): pl.pallas_call(kernel, out_shape=outs, in_specs=[SMEM] * scalars + [VMEM]...  14.4 us
    ppermute x5, waiting for transfers between devices, exchange(): lax.ppermute(value, 'seq', [(i, i ^ mask) for i in range(lax.axis_size('s...  12.8 us
    ppermute x5, starting transfers between devices, exchange(): lax.ppermute(value, 'seq', [(i, i ^ mask) for i in range(lax.axis_size('s...  6.3 us
  transfers between devices with their start and end apart: 7, of which 6 were waited for; matrix products, arithmetic and copies ran while one was open for 0% of the time, Pallas kernels for 1%

profile of v4, /device:TPU:32, one launch (start us, length us, event | category | flops | bytes accessed | tf_op | source)
XLA Modules:
  0.0 104.0 jit_solution(8694449938224112372)
XLA Ops:
  0.6 0.0 copy-start.2
  0.7 2.0 %shard_map.109 = bf16[16,32,384]{2,1,0:T(8,128)(2,1)} custom-call(bf16[192,512]{1,0:T(8,128)(2,1)} %bitcast.5, bf16[192,512]{1,0:T(8,128)(2,1)} %bitcast.6), custom_call_target="tpu_custom_call" | custom-call | tf_op jit(solution)/shard_map/pallas_call | solution.py:253
  2.7 11.3 %all-to-all-start = ((bf16[16,32,384]{2,1,0:T(8,128)(2,1)}), bf16[16,32,384]{2,1,0:T(8,128)(2,1)S(1)}, u32[]{:S(2)}, u32[]{:S(2)}) async-start(bf16[16,32,384]{2,1,0:T(8,128)(2,1)} %shard_map.109), calls=%async_computation | async-start | bytes 786432 | tf_op jit(solution)/shard_map/all_to_all | solution.py:292
  14.0 10.9 %all-to-all-done.packed = bf16[16,32,384]{2,1,0:T(8,128)(2,1)S(1)} async-done(((bf16[16,32,384]{2,1,0:T(8,128)(2,1)}), bf16[16,32,384]{2,1,0:T(8,128)(2,1)S(1)}, u32[]{:S(2)}, u32[]{:S(2)}) %all-to-all-start) | async-done | bytes 393248 | tf_op jit(solution)/shard_map/all_to_all | solution.py:292
  24.9 0.0 copy-done.3
  24.9 9.5 %shard_map.110 = (bf16[16,32,384]{2,1,0:T(8,128)(2,1)}, bf16[16,152,128]{2,1,0:T(8,128)(2,1)S(1)}, f32[16,152,128]{2,1,0:T(8,128)S(1)}) custom-call(s32[1]{0:T(128)} %bitcast.core.refs_0_, bf16[16,32,384]{2,1,0:T(8,128)(2,1)S(1)} %all-to-all-done.packed, bf16[384,768]{1,0:T(8,128)(2,1)S(1)} %copy-done, bf16[768,384]{1,0:T(8,128)(2,1)S(1)} %copy-done.1, ...), custom_call_target="tpu_custom_call" | custom-call | tf_op jit(solution)/shard_map/pallas_call | solution.py:253
  34.5 0.0 collective-permute-start
  34.5 2.0 %collective-permute-done.came = bf16[16,152,128]{2,1,0:T(8,128)(2,1)S(1)} collective-permute-done((bf16[16,152,128]{2,1,0:T(8,128)(2,1)S(1)}, bf16[16,152,128]{2,1,0:T(8,128)(2,1)S(1)}, u32[]{:S(2)}, u32[]{:S(2)}) %collective-permute-start) | collective-permute-done | bytes 622624 | tf_op jit(solution)/shard_map/ppermute | solution.py:277
  36.5 0.2 shard_map.112
  36.7 16.9 %all_to_all.20.pieces = bf16[16,152,128]{2,1,0:T(8,128)(2,1)S(1)} all-to-all(bf16[16,152,128]{2,1,0:T(8,128)(2,1)S(1)} %shard_map.112), channel_id=1, replica_groups={{198,134,70,6,196,132,68,4,194,130,66,2,192,128,64,0},{199,135,71,7,197..., dimensions={0} | all-to-all | bytes 1245184 | tf_op jit(solution)/shard_map/all_to_all | solution.py:295
  53.6 0.1 shard_map.113.own
  53.7 1.6 %collective-permute-start.1 = (bf16[152,128]{1,0:T(8,128)(2,1)S(1)}, bf16[152,128]{1,0:T(8,128)(2,1)S(1)}, u32[]{:S(2)}, u32[]{:S(2)}) collective-permute-start(bf16[152,128]{1,0:T(8,128)(2,1)S(1)} %shard_map.113.own), channel_id=1, source_target_pairs={{0,8},{1,9},{2,10},{3,11},{4,12},{5,13},{6,14},{7,15},{8,0},{9,1},... | collective-permute-start | bytes 116744 | tf_op jit(solution)/shard_map/ppermute | solution.py:277
  55.2 2.5 %collective-permute-done.1.came = bf16[152,128]{1,0:T(8,128)(2,1)S(1)} collective-permute-done((bf16[152,128]{1,0:T(8,128)(2,1)S(1)}, bf16[152,128]{1,0:T(8,128)(2,1)S(1)}, u32[]{:S(2)}, u32[]{:S(2)}) %collective-permute-start.1) | collective-permute-done | bytes 38944 | tf_op jit(solution)/shard_map/ppermute | solution.py:277
  57.8 1.1 %collective-permute-start.2 = (bf16[152,128]{1,0:T(8,128)(2,1)S(1)}, bf16[152,128]{1,0:T(8,128)(2,1)S(1)}, u32[]{:S(2)}, u32[]{:S(2)}) collective-permute-start(bf16[152,128]{1,0:T(8,128)(2,1)S(1)} %shard_map.114.own), channel_id=1, source_target_pairs={{0,16},{1,17},{2,18},{3,19},{4,20},{5,21},{6,22},{7,23},{8,24},{9,... | collective-permute-start | bytes 116744 | tf_op jit(solution)/shard_map/ppermute | solution.py:277
  58.9 3.9 %collective-permute-done.2.came = bf16[152,128]{1,0:T(8,128)(2,1)S(1)} collective-permute-done((bf16[152,128]{1,0:T(8,128)(2,1)S(1)}, bf16[152,128]{1,0:T(8,128)(2,1)S(1)}, u32[]{:S(2)}, u32[]{:S(2)}) %collective-permute-start.2) | collective-permute-done | bytes 38944 | tf_op jit(solution)/shard_map/ppermute | solution.py:277
  62.8 3.6 %collective-permute-start.3 = (bf16[152,128]{1,0:T(8,128)(2,1)S(1)}, bf16[152,128]{1,0:T(8,128)(2,1)S(1)}, u32[]{:S(2)}, u32[]{:S(2)}) collective-permute-start(bf16[152,128]{1,0:T(8,128)(2,1)S(1)} %shard_map.115.own), channel_id=1, source_target_pairs={{0,32},{1,33},{2,34},{3,35},{4,36},{5,37},{6,38},{7,39},{8,40},{9,... | collective-permute-start | bytes 116744 | tf_op jit(solution)/shard_map/ppermute | solution.py:277
  66.4 4.4 %collective-permute-done.3.came = bf16[152,128]{1,0:T(8,128)(2,1)S(1)} collective-permute-done((bf16[152,128]{1,0:T(8,128)(2,1)S(1)}, bf16[152,128]{1,0:T(8,128)(2,1)S(1)}, u32[]{:S(2)}, u32[]{:S(2)}) %collective-permute-start.3) | collective-permute-done | bytes 38944 | tf_op jit(solution)/shard_map/ppermute | solution.py:277
  70.8 13.9 %all_to_all.21.refs_2_ = bf16[16,152,128]{2,1,0:T(8,128)(2,1)S(1)} all-to-all(bf16[16,152,128]{2,1,0:T(8,128)(2,1)S(1)} %shard_map.116), channel_id=1, replica_groups={{198,134,70,6,196,132,68,4,194,130,66,2,192,128,64,0},{199,135,71,7,197..., dimensions={0} | all-to-all | bytes 1245184 | tf_op jit(solution)/shard_map/all_to_all | solution.py:295
  84.7 8.9 %all-to-all-start.1 = ((bf16[16,32,384]{2,1,0:T(8,128)(2,1)}), bf16[16,32,384]{2,1,0:T(8,128)(2,1)S(1)}, u32[]{:S(2)}, u32[]{:S(2)}) async-start(bf16[16,32,384]{2,1,0:T(8,128)(2,1)} %get-tuple-element.15), calls=%async_computation.1 | async-start | bytes 786432 | tf_op jit(solution)/shard_map/all_to_all | solution.py:292
  93.6 0.0 collective-permute-start.4
  93.6 7.9 %all-to-all-done.1.packed = bf16[16,32,384]{2,1,0:T(8,128)(2,1)S(1)} async-done(((bf16[16,32,384]{2,1,0:T(8,128)(2,1)}), bf16[16,32,384]{2,1,0:T(8,128)(2,1)S(1)}, u32[]{:S(2)}, u32[]{:S(2)}) %all-to-all-start.1) | async-done | bytes 393248 | tf_op jit(solution)/shard_map/all_to_all | solution.py:292
  101.5 0.9 shard_map.111
  102.4 0.0 collective-permute-done.4.refs_3_
  102.4 1.6 %shard_map.117 = (f32[384,768]{1,0:T(8,128)}, f32[768,384]{1,0:T(8,128)}, f32[384]{0:T(512)}, f32[384]{0:T(512)}) custom-call(s32[1]{0:T(128)} %bitcast.core.refs_0_, f32[384]{0:T(512)S(1)} %copy-done.2, bf16[16,152,128]{2,1,0:T(8,128)(2,1)S(1)} %all_to_all.21.refs_2_, bf16[16,152,128]{2,1,0:T(8,128)(2,1)S(1)} %collective-permute-done.4.refs_3_), custom_call_target="tpu_custom_call" | custom-call | tf_op jit(solution)/shard_map/pallas_call | solution.py:253
  (9 shorter events, 0.1 us)
Async XLA Ops:
  0.6 24.3 %copy-start.2 = (f32[384]{0:T(512)S(1)}, f32[384]{0:T(512)}, u32[]{:S(2)}) copy-start(f32[384]{0:T(512)} %refs_1_.1) | copy-start | bytes 4612
  0.6 24.3 %copy-start.3 = (f32[384]{0:T(512)S(1)}, f32[384]{0:T(512)}, u32[]{:S(2)}) copy-start(f32[384]{0:T(512)} %bias.1) | copy-start | bytes 4612
  0.7 24.3 %copy-start.1 = (bf16[768,384]{1,0:T(8,128)(2,1)S(1)}, bf16[768,384]{1,0:T(8,128)(2,1)}, u32[]{:S(2)}) copy-start(bf16[768,384]{1,0:T(8,128)(2,1)} %merge.1) | copy-start | bytes 1769476
  0.7 24.3 %copy-start = (bf16[384,768]{1,0:T(8,128)(2,1)S(1)}, bf16[384,768]{1,0:T(8,128)(2,1)}, u32[]{:S(2)}) copy-start(bf16[384,768]{1,0:T(8,128)(2,1)} %spread.1) | copy-start | bytes 1769476
  2.7 22.2 %all-to-all-start = ((bf16[16,32,384]{2,1,0:T(8,128)(2,1)}), bf16[16,32,384]{2,1,0:T(8,128)(2,1)S(1)}, u32[]{:S(2)}, u32[]{:S(2)}) async-start(bf16[16,32,384]{2,1,0:T(8,128)(2,1)} %shard_map.109), calls=%async_computation | async-start | bytes 786432 | tf_op jit(solution)/shard_map/all_to_all | solution.py:292
  34.5 2.1 %collective-permute-start = (bf16[16,152,128]{2,1,0:T(8,128)(2,1)S(1)}, bf16[16,152,128]{2,1,0:T(8,128)(2,1)S(1)}, u32[]{:S(2)}, u32[]{:S(2)}) collective-permute-start(bf16[16,152,128]{2,1,0:T(8,128)(2,1)S(1)} %get-tuple-element.19), channel_id=1, source_target_pairs={{0,1},{1,0},{2,3},{3,2},{4,5},{5,4},{6,7},{7,6},{8,9},{9,8},{10,11... | collective-permute-start | bytes 1867784 | tf_op jit(solution)/shard_map/ppermute | solution.py:277
  53.7 4.1 %collective-permute-start.1 = (bf16[152,128]{1,0:T(8,128)(2,1)S(1)}, bf16[152,128]{1,0:T(8,128)(2,1)S(1)}, u32[]{:S(2)}, u32[]{:S(2)}) collective-permute-start(bf16[152,128]{1,0:T(8,128)(2,1)S(1)} %shard_map.113.own), channel_id=1, source_target_pairs={{0,8},{1,9},{2,10},{3,11},{4,12},{5,13},{6,14},{7,15},{8,0},{9,1},... | collective-permute-start | bytes 116744 | tf_op jit(solution)/shard_map/ppermute | solution.py:277
  57.8 5.0 %collective-permute-start.2 = (bf16[152,128]{1,0:T(8,128)(2,1)S(1)}, bf16[152,128]{1,0:T(8,128)(2,1)S(1)}, u32[]{:S(2)}, u32[]{:S(2)}) collective-permute-start(bf16[152,128]{1,0:T(8,128)(2,1)S(1)} %shard_map.114.own), channel_id=1, source_target_pairs={{0,16},{1,17},{2,18},{3,19},{4,20},{5,21},{6,22},{7,23},{8,24},{9,... | collective-permute-start | bytes 116744 | tf_op jit(solution)/shard_map/ppermute | solution.py:277
  62.8 8.0 %collective-permute-start.3 = (bf16[152,128]{1,0:T(8,128)(2,1)S(1)}, bf16[152,128]{1,0:T(8,128)(2,1)S(1)}, u32[]{:S(2)}, u32[]{:S(2)}) collective-permute-start(bf16[152,128]{1,0:T(8,128)(2,1)S(1)} %shard_map.115.own), channel_id=1, source_target_pairs={{0,32},{1,33},{2,34},{3,35},{4,36},{5,37},{6,38},{7,39},{8,40},{9,... | collective-permute-start | bytes 116744 | tf_op jit(solution)/shard_map/ppermute | solution.py:277
  84.7 16.8 %all-to-all-start.1 = ((bf16[16,32,384]{2,1,0:T(8,128)(2,1)}), bf16[16,32,384]{2,1,0:T(8,128)(2,1)S(1)}, u32[]{:S(2)}, u32[]{:S(2)}) async-start(bf16[16,32,384]{2,1,0:T(8,128)(2,1)} %get-tuple-element.15), calls=%async_computation.1 | async-start | bytes 786432 | tf_op jit(solution)/shard_map/all_to_all | solution.py:292
  93.6 8.8 %collective-permute-start.4 = (bf16[16,152,128]{2,1,0:T(8,128)(2,1)S(1)}, bf16[16,152,128]{2,1,0:T(8,128)(2,1)S(1)}, u32[]{:S(2)}, u32[]{:S(2)}) collective-permute-start(bf16[16,152,128]{2,1,0:T(8,128)(2,1)S(1)} %all_to_all.21.refs_2_), channel_id=1, source_target_pairs={{0,1},{1,0},{2,3},{3,2},{4,5},{5,4},{6,7},{7,6},{8,9},{9,8},{10,11... | collective-permute-start | bytes 1867784 | tf_op jit(solution)/shard_map/ppermute | solution.py:277

commit v5 on v4

--- a/solution.py
+++ b/solution.py
@@ -18,6 +18,7 @@
 PIECE = 144
 AUX = 8
 BLOCK = 32
+STEPS = 2
 ORDER = list(reversed(range(MEMBERS)))
 
 sqrt_half = 0.7071067811865476
@@ -177,8 +178,8 @@
 
 def pack_kernel(tokens, out_grad, packed):
     rows = jnp.concatenate([tokens[...], out_grad[...]], 0).T
-    for i, g in enumerate(ORDER):
-        packed[i] = rows[ROWS * g : ROWS * (g + 1)]
+    for k in range(MEMBERS // STEPS):
+        packed[MEMBERS // STEPS - 1 - k] = rows[ROWS * k : ROWS * (k + 1)]
 
 
 def unpack_kernel(packed, network_out, token_grad):
@@ -205,25 +206,31 @@
 
 
 def finish_kernel(core, gate, mine, theirs, spread, merge, bias, gate_out, *, grad_scale):
+    step = pl.program_id(0)
+    each = 16 // STEPS
+
     def write(first, second):
-        for p in range(16):
-            rows = slice(24 * p, 24 * (p + 1))
+        for k in range(each):
+            rows = slice(24 * k, 24 * (k + 1))
             for c in range(6):
                 spread[rows, 128 * c : 128 * (c + 1)] = (
-                    first[p, 24 * c : 24 * (c + 1), :].astype(f32) * grad_scale
+                    first[each * step + k, 24 * c : 24 * (c + 1), :].astype(f32) * grad_scale
                 )
-            rows = slice(48 * p, 48 * (p + 1))
+            rows = slice(48 * k, 48 * (k + 1))
             for c in range(3):
                 merge[rows, 128 * c : 128 * (c + 1)] = (
-                    second[p, 48 * c : 48 * (c + 1), :].astype(f32) * grad_scale
+                    second[each * step + k, 48 * c : 48 * (c + 1), :].astype(f32) * grad_scale
                 )
-        aux = first[0, PIECE:, :].astype(f32) * grad_scale
-        gate_open = jax.nn.sigmoid(gate[...].reshape(1, SWITCH))
-        slope = gate_open * (1.0 - gate_open)
-        for k in range(3):
-            at = slice(128 * k, 128 * (k + 1))
-            bias[at] = aux[k, :]
-            gate_out[at] = aux[3 + k, :] * slope[0, at]
+
+        @pl.when(step == 0)
+        def _():
+            aux = first[0, PIECE:, :].astype(f32) * grad_scale
+            gate_open = jax.nn.sigmoid(gate[...].reshape(1, SWITCH))
+            slope = gate_open * (1.0 - gate_open)
+            for k in range(3):
+                at = slice(128 * k, 128 * (k + 1))
+                bias[at] = aux[k, :]
+                gate_out[at] = aux[3 + k, :] * slope[0, at]
 
     @pl.when(core[0] == 0)
     def _():
@@ -246,15 +253,20 @@
 SMEM = pl.BlockSpec(memory_space=pltpu.SMEM)
 
 
-def call(kernel, outs, ins, scalars=0, scratch=(), far=False):
+def call(kernel, outs, ins, scalars=0, scratch=(), far=False, grid=(), blocks=None):
     arrays = ins[scalars:]
     space = pltpu.HBM if far else pltpu.VMEM
     arrays = [pltpu.with_memory_space_constraint(a, space) for a in arrays]
     return pl.pallas_call(
         kernel,
         out_shape=outs,
-        in_specs=[SMEM] * scalars + [VMEM] * len(arrays),
-        out_specs=tuple(VMEM for _ in outs) if isinstance(outs, tuple) else VMEM,
+        grid=grid,
+        in_specs=blocks[0] if blocks else [SMEM] * scalars + [VMEM] * len(arrays),
+        out_specs=blocks[1]
+        if blocks
+        else tuple(VMEM for _ in outs)
+        if isinstance(outs, tuple)
+        else VMEM,
         scratch_shapes=list(scratch),
         compiler_params=pltpu.CompilerParams(vmem_limit_bytes=40 * 2**20),
     )(*ins[:scalars], *arrays)
@@ -300,6 +312,11 @@
         near((MEMBERS, ROWS, SWITCH), bf16),
         (tokens.T, out_grad.T),
         far=True,
+        grid=(STEPS,),
+        blocks=(
+            [pl.BlockSpec((UNITS, rows // STEPS), lambda i: (0, i))] * 2,
+            pl.BlockSpec((MEMBERS // STEPS, ROWS, SWITCH), lambda i: (STEPS - 1 - i, 0, 0)),
+        ),
     )
     packed = swap_rows(packed)
     total = SECTIONS * PAIRS
@@ -338,9 +355,7 @@
     pieces = call(pair_sum_kernel, near(half, bf16), (summed, came))
     mine = swap_slots(pieces)
     theirs = exchange(mine, 1)
-    network_out, token_grad = call(
-        unpack_kernel, (shaped((UNITS, rows), bf16),) * 2, (packed_out,)
-    )
+    network_out, token_grad = call(unpack_kernel, (shaped((UNITS, rows), bf16),) * 2, (packed_out,))
     spread_grad, merge_grad, bias_grad, gate_grad = call(
         lambda *refs: finish_kernel(*refs, grad_scale=grad_scale),
         (
@@ -351,6 +366,16 @@
         ),
         (core, gate_logit, mine, theirs),
         1,
+        grid=(STEPS,),
+        blocks=(
+            [SMEM, VMEM, VMEM, VMEM],
+            (
+                pl.BlockSpec((SWITCH // STEPS, HIDDEN), lambda i: (i, 0)),
+                pl.BlockSpec((HIDDEN // STEPS, SWITCH), lambda i: (i, 0)),
+                pl.BlockSpec((SWITCH,), lambda i: (0,)),
+                pl.BlockSpec((SWITCH,), lambda i: (0,)),
+            ),
+        ),
     )
     return (network_out.T, token_grad.T, spread_grad, merge_grad, bias_grad, gate_grad)
 

time: 105 us -> 105 us (level)
  no operation moved by 1% of the time
where the time goes in v5:
time: 105 us; the launch traced here: 104 us
  waiting for transfers between devices  31.8 us (30%)
  blocking collectives  30.8 us (29%)
  starting transfers between devices  26.5 us (25%)
  Pallas kernels  14.2 us (14%)
    all_to_all x2, blocking collectives, swap_slots(): return lax.all_to_all(slots, 'seq', 0, 0, axis_index_groups=planes)  30.8 us
    all_to_all x2, starting transfers between devices, swap_rows(): return lax.all_to_all(packed, 'seq', 0, 0, axis_index_groups=members)  20.2 us
    all_to_all x2, waiting for transfers between devices, swap_rows(): return lax.all_to_all(packed, 'seq', 0, 0, axis_index_groups=members)  19 us
    pallas_call x9, Pallas kernels, call(): pl.pallas_call(kernel, out_shape=outs, grid=grid, in_specs=blocks[0] if b...  14.2 us
    ppermute x5, waiting for transfers between devices, exchange(): lax.ppermute(value, 'seq', [(i, i ^ mask) for i in range(lax.axis_size('s...  12.8 us
    ppermute x5, starting transfers between devices, exchange(): lax.ppermute(value, 'seq', [(i, i ^ mask) for i in range(lax.axis_size('s...  6.31 us
  transfers between devices with their start and end apart: 7, of which 6 were waited for; matrix products, arithmetic and copies ran while one was open for 0% of the time, Pallas kernels for 1%

profile of v5, /device:TPU:32, one launch (start us, length us, event | category | flops | bytes accessed | tf_op | source)
XLA Modules:
  0.0 104.0 jit_solution(10993504189595600979)
XLA Ops:
  0.6 0.0 copy-start.2
  0.7 2.0 %shard_map.109 = bf16[16,32,384]{2,1,0:T(8,128)(2,1)} custom-call(bf16[192,512]{1,0:T(8,128)(2,1)} %bitcast.5, bf16[192,512]{1,0:T(8,128)(2,1)} %bitcast.6), custom_call_target="tpu_custom_call" | custom-call | tf_op jit(solution)/shard_map/pallas_call | solution.py:260
  2.6 11.3 %all-to-all-start = ((bf16[16,32,384]{2,1,0:T(8,128)(2,1)}), bf16[16,32,384]{2,1,0:T(8,128)(2,1)S(1)}, u32[]{:S(2)}, u32[]{:S(2)}) async-start(bf16[16,32,384]{2,1,0:T(8,128)(2,1)} %shard_map.109), calls=%async_computation | async-start | bytes 786432 | tf_op jit(solution)/shard_map/all_to_all | solution.py:304
  13.9 10.9 %all-to-all-done.packed = bf16[16,32,384]{2,1,0:T(8,128)(2,1)S(1)} async-done(((bf16[16,32,384]{2,1,0:T(8,128)(2,1)}), bf16[16,32,384]{2,1,0:T(8,128)(2,1)S(1)}, u32[]{:S(2)}, u32[]{:S(2)}) %all-to-all-start) | async-done | bytes 393248 | tf_op jit(solution)/shard_map/all_to_all | solution.py:304
  24.8 0.0 copy-done.3
  24.9 9.5 %shard_map.110 = (bf16[16,32,384]{2,1,0:T(8,128)(2,1)}, bf16[16,152,128]{2,1,0:T(8,128)(2,1)S(1)}, f32[16,152,128]{2,1,0:T(8,128)S(1)}) custom-call(s32[1]{0:T(128)} %bitcast.core.refs_0_, bf16[16,32,384]{2,1,0:T(8,128)(2,1)S(1)} %all-to-all-done.packed, bf16[384,768]{1,0:T(8,128)(2,1)S(1)} %copy-done, bf16[768,384]{1,0:T(8,128)(2,1)S(1)} %copy-done.1, ...), custom_call_target="tpu_custom_call" | custom-call | tf_op jit(solution)/shard_map/pallas_call | solution.py:260
  34.4 0.0 collective-permute-start
  34.4 2.0 %collective-permute-done.came = bf16[16,152,128]{2,1,0:T(8,128)(2,1)S(1)} collective-permute-done((bf16[16,152,128]{2,1,0:T(8,128)(2,1)S(1)}, bf16[16,152,128]{2,1,0:T(8,128)(2,1)S(1)}, u32[]{:S(2)}, u32[]{:S(2)}) %collective-permute-start) | collective-permute-done | bytes 622624 | tf_op jit(solution)/shard_map/ppermute | solution.py:289
  36.5 0.2 shard_map.112
  36.6 16.9 %all_to_all.20.pieces = bf16[16,152,128]{2,1,0:T(8,128)(2,1)S(1)} all-to-all(bf16[16,152,128]{2,1,0:T(8,128)(2,1)S(1)} %shard_map.112), channel_id=1, replica_groups={{198,134,70,6,196,132,68,4,194,130,66,2,192,128,64,0},{199,135,71,7,197..., dimensions={0} | all-to-all | bytes 1245184 | tf_op jit(solution)/shard_map/all_to_all | solution.py:307
  53.5 0.1 shard_map.113.own
  53.6 1.6 %collective-permute-start.1 = (bf16[152,128]{1,0:T(8,128)(2,1)S(1)}, bf16[152,128]{1,0:T(8,128)(2,1)S(1)}, u32[]{:S(2)}, u32[]{:S(2)}) collective-permute-start(bf16[152,128]{1,0:T(8,128)(2,1)S(1)} %shard_map.113.own), channel_id=1, source_target_pairs={{0,8},{1,9},{2,10},{3,11},{4,12},{5,13},{6,14},{7,15},{8,0},{9,1},... | collective-permute-start | bytes 116744 | tf_op jit(solution)/shard_map/ppermute | solution.py:289
  55.2 2.5 %collective-permute-done.1.came = bf16[152,128]{1,0:T(8,128)(2,1)S(1)} collective-permute-done((bf16[152,128]{1,0:T(8,128)(2,1)S(1)}, bf16[152,128]{1,0:T(8,128)(2,1)S(1)}, u32[]{:S(2)}, u32[]{:S(2)}) %collective-permute-start.1) | collective-permute-done | bytes 38944 | tf_op jit(solution)/shard_map/ppermute | solution.py:289
  57.7 1.1 %collective-permute-start.2 = (bf16[152,128]{1,0:T(8,128)(2,1)S(1)}, bf16[152,128]{1,0:T(8,128)(2,1)S(1)}, u32[]{:S(2)}, u32[]{:S(2)}) collective-permute-start(bf16[152,128]{1,0:T(8,128)(2,1)S(1)} %shard_map.114.own), channel_id=1, source_target_pairs={{0,16},{1,17},{2,18},{3,19},{4,20},{5,21},{6,22},{7,23},{8,24},{9,... | collective-permute-start | bytes 116744 | tf_op jit(solution)/shard_map/ppermute | solution.py:289
  58.8 3.9 %collective-permute-done.2.came = bf16[152,128]{1,0:T(8,128)(2,1)S(1)} collective-permute-done((bf16[152,128]{1,0:T(8,128)(2,1)S(1)}, bf16[152,128]{1,0:T(8,128)(2,1)S(1)}, u32[]{:S(2)}, u32[]{:S(2)}) %collective-permute-start.2) | collective-permute-done | bytes 38944 | tf_op jit(solution)/shard_map/ppermute | solution.py:289
  62.7 3.6 %collective-permute-start.3 = (bf16[152,128]{1,0:T(8,128)(2,1)S(1)}, bf16[152,128]{1,0:T(8,128)(2,1)S(1)}, u32[]{:S(2)}, u32[]{:S(2)}) collective-permute-start(bf16[152,128]{1,0:T(8,128)(2,1)S(1)} %shard_map.115.own), channel_id=1, source_target_pairs={{0,32},{1,33},{2,34},{3,35},{4,36},{5,37},{6,38},{7,39},{8,40},{9,... | collective-permute-start | bytes 116744 | tf_op jit(solution)/shard_map/ppermute | solution.py:289
  66.3 4.4 %collective-permute-done.3.came = bf16[152,128]{1,0:T(8,128)(2,1)S(1)} collective-permute-done((bf16[152,128]{1,0:T(8,128)(2,1)S(1)}, bf16[152,128]{1,0:T(8,128)(2,1)S(1)}, u32[]{:S(2)}, u32[]{:S(2)}) %collective-permute-start.3) | collective-permute-done | bytes 38944 | tf_op jit(solution)/shard_map/ppermute | solution.py:289
  70.8 13.9 %all_to_all.21.refs_2_ = bf16[16,152,128]{2,1,0:T(8,128)(2,1)S(1)} all-to-all(bf16[16,152,128]{2,1,0:T(8,128)(2,1)S(1)} %shard_map.116), channel_id=1, replica_groups={{198,134,70,6,196,132,68,4,194,130,66,2,192,128,64,0},{199,135,71,7,197..., dimensions={0} | all-to-all | bytes 1245184 | tf_op jit(solution)/shard_map/all_to_all | solution.py:307
  84.6 8.9 %all-to-all-start.1 = ((bf16[16,32,384]{2,1,0:T(8,128)(2,1)}), bf16[16,32,384]{2,1,0:T(8,128)(2,1)S(1)}, u32[]{:S(2)}, u32[]{:S(2)}) async-start(bf16[16,32,384]{2,1,0:T(8,128)(2,1)} %get-tuple-element.15), calls=%async_computation.1 | async-start | bytes 786432 | tf_op jit(solution)/shard_map/all_to_all | solution.py:304
  93.5 0.0 collective-permute-start.4
  93.5 8.0 %all-to-all-done.1.packed = bf16[16,32,384]{2,1,0:T(8,128)(2,1)S(1)} async-done(((bf16[16,32,384]{2,1,0:T(8,128)(2,1)}), bf16[16,32,384]{2,1,0:T(8,128)(2,1)S(1)}, u32[]{:S(2)}, u32[]{:S(2)}) %all-to-all-start.1) | async-done | bytes 393248 | tf_op jit(solution)/shard_map/all_to_all | solution.py:304
  101.6 0.9 shard_map.111
  102.4 0.0 collective-permute-done.4.refs_3_
  102.5 1.5 %shard_map.117 = (f32[384,768]{1,0:T(8,128)}, f32[768,384]{1,0:T(8,128)}, f32[384]{0:T(512)}, f32[384]{0:T(512)}) custom-call(s32[1]{0:T(128)} %bitcast.core.refs_0_, f32[384]{0:T(512)S(1)} %copy-done.2, bf16[16,152,128]{2,1,0:T(8,128)(2,1)S(1)} %all_to_all.21.refs_2_, bf16[16,152,128]{2,1,0:T(8,128)(2,1)S(1)} %collective-permute-done.4.refs_3_), custom_call_target="tpu_custom_call" | custom-call | tf_op jit(solution)/shard_map/pallas_call | solution.py:260
  (9 shorter events, 0.1 us)
Async XLA Ops:
  0.6 24.2 %copy-start.2 = (f32[384]{0:T(512)S(1)}, f32[384]{0:T(512)}, u32[]{:S(2)}) copy-start(f32[384]{0:T(512)} %refs_1_.1) | copy-start | bytes 4612
  0.6 24.2 %copy-start.3 = (f32[384]{0:T(512)S(1)}, f32[384]{0:T(512)}, u32[]{:S(2)}) copy-start(f32[384]{0:T(512)} %bias.1) | copy-start | bytes 4612
  0.7 24.2 %copy-start.1 = (bf16[768,384]{1,0:T(8,128)(2,1)S(1)}, bf16[768,384]{1,0:T(8,128)(2,1)}, u32[]{:S(2)}) copy-start(bf16[768,384]{1,0:T(8,128)(2,1)} %merge.1) | copy-start | bytes 1769476
  0.7 24.2 %copy-start = (bf16[384,768]{1,0:T(8,128)(2,1)S(1)}, bf16[384,768]{1,0:T(8,128)(2,1)}, u32[]{:S(2)}) copy-start(bf16[384,768]{1,0:T(8,128)(2,1)} %spread.1) | copy-start | bytes 1769476
  2.6 22.2 %all-to-all-start = ((bf16[16,32,384]{2,1,0:T(8,128)(2,1)}), bf16[16,32,384]{2,1,0:T(8,128)(2,1)S(1)}, u32[]{:S(2)}, u32[]{:S(2)}) async-start(bf16[16,32,384]{2,1,0:T(8,128)(2,1)} %shard_map.109), calls=%async_computation | async-start | bytes 786432 | tf_op jit(solution)/shard_map/all_to_all | solution.py:304
  34.4 2.1 %collective-permute-start = (bf16[16,152,128]{2,1,0:T(8,128)(2,1)S(1)}, bf16[16,152,128]{2,1,0:T(8,128)(2,1)S(1)}, u32[]{:S(2)}, u32[]{:S(2)}) collective-permute-start(bf16[16,152,128]{2,1,0:T(8,128)(2,1)S(1)} %get-tuple-element.19), channel_id=1, source_target_pairs={{0,1},{1,0},{2,3},{3,2},{4,5},{5,4},{6,7},{7,6},{8,9},{9,8},{10,11... | collective-permute-start | bytes 1867784 | tf_op jit(solution)/shard_map/ppermute | solution.py:289
  53.6 4.1 %collective-permute-start.1 = (bf16[152,128]{1,0:T(8,128)(2,1)S(1)}, bf16[152,128]{1,0:T(8,128)(2,1)S(1)}, u32[]{:S(2)}, u32[]{:S(2)}) collective-permute-start(bf16[152,128]{1,0:T(8,128)(2,1)S(1)} %shard_map.113.own), channel_id=1, source_target_pairs={{0,8},{1,9},{2,10},{3,11},{4,12},{5,13},{6,14},{7,15},{8,0},{9,1},... | collective-permute-start | bytes 116744 | tf_op jit(solution)/shard_map/ppermute | solution.py:289
  57.7 5.0 %collective-permute-start.2 = (bf16[152,128]{1,0:T(8,128)(2,1)S(1)}, bf16[152,128]{1,0:T(8,128)(2,1)S(1)}, u32[]{:S(2)}, u32[]{:S(2)}) collective-permute-start(bf16[152,128]{1,0:T(8,128)(2,1)S(1)} %shard_map.114.own), channel_id=1, source_target_pairs={{0,16},{1,17},{2,18},{3,19},{4,20},{5,21},{6,22},{7,23},{8,24},{9,... | collective-permute-start | bytes 116744 | tf_op jit(solution)/shard_map/ppermute | solution.py:289
  62.7 8.0 %collective-permute-start.3 = (bf16[152,128]{1,0:T(8,128)(2,1)S(1)}, bf16[152,128]{1,0:T(8,128)(2,1)S(1)}, u32[]{:S(2)}, u32[]{:S(2)}) collective-permute-start(bf16[152,128]{1,0:T(8,128)(2,1)S(1)} %shard_map.115.own), channel_id=1, source_target_pairs={{0,32},{1,33},{2,34},{3,35},{4,36},{5,37},{6,38},{7,39},{8,40},{9,... | collective-permute-start | bytes 116744 | tf_op jit(solution)/shard_map/ppermute | solution.py:289
  84.6 16.9 %all-to-all-start.1 = ((bf16[16,32,384]{2,1,0:T(8,128)(2,1)}), bf16[16,32,384]{2,1,0:T(8,128)(2,1)S(1)}, u32[]{:S(2)}, u32[]{:S(2)}) async-start(bf16[16,32,384]{2,1,0:T(8,128)(2,1)} %get-tuple-element.15), calls=%async_computation.1 | async-start | bytes 786432 | tf_op jit(solution)/shard_map/all_to_all | solution.py:304
  93.5 8.9 %collective-permute-start.4 = (bf16[16,152,128]{2,1,0:T(8,128)(2,1)S(1)}, bf16[16,152,128]{2,1,0:T(8,128)(2,1)S(1)}, u32[]{:S(2)}, u32[]{:S(2)}) collective-permute-start(bf16[16,152,128]{2,1,0:T(8,128)(2,1)S(1)} %all_to_all.21.refs_2_), channel_id=1, source_target_pairs={{0,1},{1,0},{2,3},{3,2},{4,5},{5,4},{6,7},{7,6},{8,9},{9,8},{10,11... | collective-permute-start | bytes 1867784 | tf_op jit(solution)/shard_map/ppermute | solution.py:289
